TPU v7x, 128 devices: a whole 4x4x4 slice. The times are simulated.
128 devices in a mesh: side: 2 (over x_lo), seq: 16 (over y, x_hi, core), head: 4 (over z).
Axes of the slice: x: 4 (x_hi: 2, x_lo: 2; x = x_hi * 2 + x_lo), y: 4, z: 4, core: 2. Of those that a mesh axis runs over, the one named last changes fastest.
Arguments:
- cached_hidden: bfloat16 [8, 12288, 8192], P('side', ('seq', 'head')), may hold values from -240 to 240
- page_order: int32 [8, 768], P('side', ('seq', 'head')), may hold values from 0 to 11, as said below
- lengths: int32 [8], P('side'), may hold values from 3072 to 12288, as said below
- new_ids: int32 [8, 4], replicated, may hold values from 0 to 64511
- embedding: bfloat16 [64512, 8192], P('side', ('seq', 'head')), may hold values from -128 to 128
- query_proj: bfloat16 [8192, 8192], P(('seq', 'head')), may hold values from -0.15625 to 0.15625
- down_proj: bfloat16 [8192, 1024], P(('seq', 'head')), may hold values from -0.0625 to 0.0625
- key_up: bfloat16 [8, 64, 128], P('head'), may hold values from -0.75 to 0.75
- value_up: bfloat16 [8, 64, 128], P('head'), may hold values from -1.5 to 1.5
- out_proj: bfloat16 [8192, 8192], P('head', 'seq'), may hold values from -0.0625 to 0.0625
Outputs:
- attended: bfloat16 [8, 4, 8192], P('side', None, 'seq')
Inputs may be any that keep to these rules, and one draw needn't show every extreme that they name: `lengths`: each request's number of cached tokens; in every draw some request has exactly 12288. `page_order`: in each row every aligned run of 12 entries holds each number once; entry j of run b names the page of run b's 192 positions in which the request's logical page j of that run is stored.
All inputs are finite; a program needn't handle non-finite values.
Results may differ from a plain program's by a relative error of at most 0.012.
The roundings to bfloat16 on the way count: a program that leaves them out, or rounds other values in their place, can miss the bound.
Values may be sent and summed in bfloat16 or wider, within the bound.
A program may use at most 128 MiB of HBM per device.

v0:
```python
import math

import jax
import jax.numpy as jnp
from jax import lax
from jax.sharding import Mesh
from jax.sharding import PartitionSpec as P

D = 8192
HQ = 64
KVH = 8
HD = 128
PAGE = 16
SEQ = ("seq_0", "seq_1", "seq_2")
SIDE_SEQ_HEAD = ("side", "seq_0", "seq_1", "seq_2", "head")
SEQ_HEAD = ("seq_0", "seq_1", "seq_2", "head")


rope_base = 500000.0
masked_score = -1e30


def all_in_one(array, axis):
    leaves = jax.tree.leaves(array)
    sequence = sorted(range(len(leaves)), key=lambda k: -leaves[k].size)
    width = (1, *leaves[sequence[0]].shape)[-1]
    lines = [
        jnp.pad(leaves[k].reshape(-1), (0, -leaves[k].size % width)).reshape(-1, width)
        for k in sequence
    ]
    both, at, found = (lax.all_gather(jnp.concatenate(lines), axis), 0, {})
    for k, line in zip(sequence, lines):
        section = both[:, at : at + len(line)].reshape(len(both), -1)
        found[k] = section[:, : leaves[k].size].reshape(-1, *leaves[k].shape)
        at += len(line)
    numbers = iter(range(len(leaves)))
    return jax.tree.map(lambda _: found[next(numbers)], array)


def joined_all(array, axes, combine):
    for axis in axes:
        pieces = all_in_one(array, axis)
        array = jax.tree.map(lambda part: part[0], pieces)
        for k in range(1, lax.axis_size(axis)):
            array = combine(array, jax.tree.map(lambda part: part[k], pieces))
    return array


def sent_to_all(array, axis):
    devices = lax.axis_size(axis)
    return lax.all_to_all(
        jnp.broadcast_to(array[None], (devices, *array.shape)), axis, 0, 0, tiled=True
    )


def taken_together(array, axis):
    everything = sent_to_all(array, axis)
    return jnp.sum(everything, axis=0)


def rotate(values, positions):
    half_width = values.shape[-1] // 2
    frequency = 1.0 / rope_base ** (
        jnp.arange(half_width, dtype=jnp.float32) * 2.0 / values.shape[-1]
    )
    angles = positions.astype(jnp.float32)[..., None] * frequency
    cosine = jnp.cos(angles)
    sines = jnp.sin(angles)
    lower_half = values[..., :half_width]
    upper_half = values[..., half_width:]
    return jnp.concatenate(
        [lower_half * cosine - upper_half * sines, upper_half * cosine + lower_half * sines],
        axis=-1,
    )


def rebuild(latent, positions, key_up, value_up):
    latent_rank = key_up.shape[1]
    rebuilt_keys = jnp.einsum(
        "...gc,gcd->...gd", latent[..., :latent_rank], key_up, preferred_element_type=jnp.float32
    )
    rebuilt_keys = rotate(rebuilt_keys, positions[..., None]).astype(jnp.bfloat16)
    rebuilt_values = jnp.einsum(
        "...gc,gcd->...gd", latent[..., latent_rank:], value_up, preferred_element_type=jnp.float32
    )
    return (rebuilt_keys, rebuilt_values.astype(jnp.bfloat16))


def combine(earlier, latter):
    peak_early, total_early, summed_early = earlier
    peak_late, total_late, summed_late = latter
    joint_peak = jnp.maximum(peak_early, peak_late)
    weight_early = jnp.exp(peak_early - joint_peak)
    weight_late = jnp.exp(peak_late - joint_peak)
    joint_total = total_early * weight_early + total_late * weight_late
    joint_summed = summed_early * weight_early[..., None] + summed_late * weight_late[..., None]
    return (joint_peak, joint_total, joint_summed)


def local(
    cached_hidden,
    page_order,
    lengths,
    new_ids,
    embedding,
    query_proj,
    down_proj,
    key_up,
    value_up,
    out_proj,
):
    req_side, len_dev, model_width = cached_hidden.shape
    vocab_half = embedding.shape[0]
    side_index = lax.axis_index("side")
    seq_index = lax.axis_index(SEQ)
    head_index = lax.axis_index("head")
    head_count = lax.axis_size("head")
    requests, steps = new_ids.shape
    local_ids = new_ids.reshape(-1) - side_index * vocab_half
    inside = (local_ids >= 0) & (local_ids < vocab_half)
    picked = jnp.take(embedding, jnp.clip(local_ids, 0, vocab_half - 1), axis=0)
    picked = jnp.where(inside[:, None], picked, jnp.zeros_like(picked))
    query_part = jnp.dot(picked, query_proj, preferred_element_type=jnp.float32).reshape(
        requests, steps, -1
    )
    latent_part = jnp.dot(picked, down_proj, preferred_element_type=jnp.float32).reshape(
        requests, steps, -1
    )
    widened = picked.astype(jnp.float32)
    square_part = jnp.sum(widened * widened, axis=-1).reshape(requests, steps)
    query_all, latent_all, square_all = lax.psum(
        (query_part, latent_part, square_part), SIDE_SEQ_HEAD
    )
    first_request = side_index * req_side
    query_sum = lax.dynamic_slice_in_dim(query_all, first_request, req_side, 0)
    latent_sum = lax.dynamic_slice_in_dim(latent_all, first_request, req_side, 0)
    square_sum = lax.dynamic_slice_in_dim(square_all, first_request, req_side, 0)
    inv_rms = lax.rsqrt(square_sum / D + 1e-05)
    local_heads = HQ // head_count
    local_groups = key_up.shape[0]
    latent_width = down_proj.shape[1] // KVH
    query_cols = lax.dynamic_slice_in_dim(
        query_sum, head_index * local_heads * HD, local_heads * HD, 2
    )
    query_cols = query_cols.reshape(req_side, steps, local_heads, HD) * inv_rms[:, :, None, None]
    fresh_positions = lengths[:, None] + jnp.arange(steps, dtype=jnp.int32)[None, :]
    queries = rotate(query_cols, fresh_positions[..., None]).astype(jnp.bfloat16)
    queries = queries.reshape(req_side, steps, local_groups, local_heads // local_groups, HD)
    fresh_cols = lax.dynamic_slice_in_dim(
        latent_sum, head_index * local_groups * latent_width, local_groups * latent_width, 2
    )
    fresh_latent = (
        fresh_cols.reshape(req_side, steps, local_groups, latent_width) * inv_rms[:, :, None, None]
    ).astype(jnp.bfloat16)
    fresh_keys, fresh_values = rebuild(fresh_latent, fresh_positions, key_up, value_up)
    token_rows = cached_hidden.reshape(req_side * len_dev, model_width)
    latent = jnp.dot(
        token_rows,
        lax.all_gather(down_proj, SEQ_HEAD, axis=0, tiled=True),
        preferred_element_type=jnp.float32,
    )
    latent = latent.astype(jnp.bfloat16)
    pages = len_dev // PAGE
    page_rows = latent.reshape(req_side * pages, PAGE * latent.shape[-1])
    wanted = (jnp.arange(req_side, dtype=jnp.int32)[:, None] * pages + page_order).reshape(-1)
    ordered = jnp.take(page_rows, wanted, axis=0).reshape(req_side, len_dev, KVH, latent_width)
    received = lax.all_to_all(ordered, "head", split_axis=2, concat_axis=1, tiled=True)
    span = received.shape[1]
    positions = seq_index * span + jnp.arange(span, dtype=jnp.int32)
    cache_keys, cache_values = rebuild(received, positions, key_up, value_up)
    scaling = 1.0 / math.sqrt(HD)
    cache_scores = (
        jnp.einsum("rtgjd,rpgd->rtgjp", queries, cache_keys, preferred_element_type=jnp.float32)
        * scaling
    )
    fresh_scores = (
        jnp.einsum("rtgjd,rugd->rtgju", queries, fresh_keys, preferred_element_type=jnp.float32)
        * scaling
    )
    live = (positions[None, :] < lengths[:, None])[:, None, None, None, :]
    causal = (jnp.arange(steps)[:, None] >= jnp.arange(steps)[None, :]) & (seq_index == 0)
    seen = causal[None, :, None, None, :]
    cache_scores = jnp.where(live, cache_scores, masked_score)
    fresh_scores = jnp.where(seen, fresh_scores, masked_score)
    row_peak = jnp.maximum(jnp.max(cache_scores, axis=-1), jnp.max(fresh_scores, axis=-1))
    cache_weights = jnp.where(live, jnp.exp(cache_scores - row_peak[..., None]), 0.0)
    fresh_weights = jnp.where(seen, jnp.exp(fresh_scores - row_peak[..., None]), 0.0)
    totals = jnp.sum(cache_weights, axis=-1) + jnp.sum(fresh_weights, axis=-1)
    summed = jnp.einsum(
        "rtgjp,rpgd->rtgjd",
        cache_weights.astype(jnp.bfloat16),
        cache_values,
        preferred_element_type=jnp.float32,
    )
    summed = summed + jnp.einsum(
        "rtgju,rugd->rtgjd",
        fresh_weights.astype(jnp.bfloat16),
        fresh_values,
        preferred_element_type=jnp.float32,
    )
    row_peak, totals, summed = joined_all((row_peak, totals, summed), SEQ, combine)
    context = (summed / totals[..., None]).astype(jnp.bfloat16).reshape(req_side * steps, -1)
    partial_out = jnp.dot(context, out_proj, preferred_element_type=jnp.float32)
    attended = taken_together(partial_out, "head")
    return attended.astype(jnp.bfloat16).reshape(req_side, steps, -1)


def solution(mesh):
    finer = Mesh(
        mesh.devices.reshape(mesh.shape["side"], 4, 2, 2, mesh.shape["head"]),
        ("side", "seq_0", "seq_1", "seq_2", "head"),
    )
    placed = (
        P("side", SEQ_HEAD, None),
        P("side", SEQ_HEAD),
        P("side"),
        P(),
        P("side", SEQ_HEAD),
        P(SEQ_HEAD, None),
        P(SEQ_HEAD, None),
        P("head", None, None),
        P("head", None, None),
        P("head", SEQ),
    )
    return jax.shard_map(
        local, mesh=finer, in_specs=placed, out_specs=P("side", None, SEQ), check_vma=False
    )
```

profile of v0, /device:TPU:1, one launch (start us, length us, event | category | flops | bytes accessed | tf_op | source)
XLA Modules:
  0.0 303.7 jit_solution(17250674614541638351)
XLA Ops:
  7.4 0.8 compare_and_fusion.1
  9.4 5.0 %gather_fusion.1 = bf16[32,128]{1,0:T(8,128)(2,1)S(1)} fusion(bf16[32256,128]{1,0:T(8,128)(2,1)} %param.14, s32[1024]{0:T(1024)S(1)} %pad_clamp_fusion), kind=kCustom, calls=%fused_computation.1 | custom fusion | bytes 16512 | tf_op jit(solution)/shard_map/jit(_take)/gather | solution.py:121
  14.4 1.2 fusion.108
  16.7 1.3 reshape.581
  18.8 72.1 %psum.22 = f32[8,4]{1,0:T(8,128)S(1)} all-reduce(f32[8,4]{1,0:T(8,128)S(1)} %reshape.583), channel_id=1, replica_groups=mesh['side'=2,'seq_0'=4,'seq_1'=2,'seq_2'=2,'head'=4] {'side','seq_0','s..., use_global_device_ids=true, to_apply=%region_2.3 | all-reduce | flops 32 | bytes 256 | tf_op jit(solution)/shard_map/psum | solution.py:131
  94.4 0.7 multiply_cosine_fusion.1
  95.2 0.8 multiply_cosine_fusion
  95.9 111.3 %all-reduce.3.cloned.1.call-done = (f32[8,4,8192]{2,1,0:T(4,128)}, f32[8,4,1024]{2,1,0:T(4,128)}) async-done(((f32[8,4,8192]{2,1,0:T(4,128)}, f32[8,4,1024]{2,1,0:T(4,128)}), (f32[8,4,8192]{2,1,0:T(4,128)}, f32[8,4,1024]{2,1,0:T(4,128)})) %all-reduce.3.cloned.1.call-update) | async-done | bytes 1179664 | tf_op jit(solution)/shard_map/psum | solution.py:131
  207.3 1.7 constant_dynamic-slice_fusion
  209.0 18.7 %convolution_convert_fusion.1 = bf16[768,1024]{1,0:T(8,128)(2,1)S(1)} fusion(bf16[768,8192]{1,0:T(8,128)(2,1)} %bitcast.293, bf16[8192,1024]{1,0:T(8,128)(2,1)} %all-gather.8.cloned.1.call-done), kind=kOutput, calls=%fused_computation.4 | convolution fusion | flops 12885688320 | bytes 30932992 | tf_op jit(solution)/shard_map/dot_general | solution.py:157
  227.7 0.8 reshape.579
  228.5 1.7 gather_fusion
  230.2 0.8 gather.11
  231.0 1.4 copy_select_fusion
  232.5 3.9 %all-to-all-start = ((bf16[4,192,8,128]{3,1,0,2:T(8,128)(2,1)}), bf16[4,192,8,128]{3,1,0,2:T(8,128)(2,1)S(1)}, u32[]{:S(2)}, u32[]{:S(2)}) async-start(bf16[4,192,8,128]{3,1,0,2:T(8,128)(2,1)} %copy_select_fusion), calls=%async_computation | async-start | bytes 3145728 | tf_op jit(solution)/shard_map/all_to_all | solution.py:167
  236.4 0.8 fusion.70
  237.8 1.7 fusion.115
  239.5 16.5 %all-to-all-done = bf16[4,192,8,128]{3,1,0,2:T(8,128)(2,1)S(1)} async-done(((bf16[4,192,8,128]{3,1,0,2:T(8,128)(2,1)}), bf16[4,192,8,128]{3,1,0,2:T(8,128)(2,1)S(1)}, u32[]{:S(2)}, u32[]{:S(2)}) %all-to-all-start) | async-done | bytes 1572896 | tf_op jit(solution)/shard_map/all_to_all | solution.py:167
  260.0 0.9 fusion.24
  261.0 10.3 %all-gather.3 = f32[4,260,128]{2,1,0:T(8,128)S(1)} all-gather(f32[1,260,128]{2,1,0:T(8,128)S(1)} %maximum_bitcast_fusion.1), channel_id=2, replica_groups=mesh['side'=2,'seq_0'=4,'seq_1'=2,'seq_2'=2,'head'=4] {'seq_0'}, dimensions={0}, use_global_device_ids=true | all-gather | bytes 665600 | tf_op jit(solution)/shard_map/all_gather | solution.py:31
  271.6 6.0 %all-gather.4 = f32[2,260,128]{2,1,0:T(8,128)S(1)} all-gather(f32[1,260,128]{2,1,0:T(8,128)S(1)} %maximum_bitcast_fusion.2), channel_id=3, replica_groups=mesh['side'=2,'seq_0'=4,'seq_1'=2,'seq_2'=2,'head'=4] {'seq_1'}, dimensions={0}, use_global_device_ids=true | all-gather | bytes 399360 | tf_op jit(solution)/shard_map/all_gather | solution.py:31
  277.8 7.5 %all-gather.5 = f32[2,260,128]{2,1,0:T(8,128)S(1)} all-gather(f32[1,260,128]{2,1,0:T(8,128)S(1)} %maximum_bitcast_fusion.3), channel_id=4, replica_groups=mesh['side'=2,'seq_0'=4,'seq_1'=2,'seq_2'=2,'head'=4] {'seq_2'}, dimensions={0}, use_global_device_ids=true | all-gather | bytes 399360 | tf_op jit(solution)/shard_map/all_gather | solution.py:31
  286.2 2.1 fusion.53
  288.4 7.2 %all_to_all.23 = f32[4,16,512]{2,1,0:T(8,128)S(1)} all-to-all(f32[4,16,512]{2,1,0:T(8,128)S(1)} %broadcast_in_dim.132), channel_id=1, replica_groups=mesh['side'=2,'seq_0'=4,'seq_1'=2,'seq_2'=2,'head'=4] {'head'}, dimensions={0} | all-to-all | bytes 262144 | tf_op jit(solution)/shard_map/all_to_all | solution.py:51
  (119 shorter events, 13.1 us)
Async XLA Ops:
  7.4 8.8 %copy-start = (bf16[128,8192]{1,0:T(8,128)(2,1)S(1)}, bf16[128,8192]{1,0:T(8,128)(2,1)}, u32[]{:S(2)}) copy-start(bf16[128,8192]{1,0:T(8,128)(2,1)} %param.15) | copy-start | bytes 6291460
  7.4 199.9 %all-reduce.3.cloned.1.call-start = ((), (), s32[]{:S(2)}) async-start(), calls=%async_computation.3 | async-start | bytes 2359296 | tf_op jit(solution)/shard_map/psum | solution.py:131
  16.7 74.3 %copy-start.18 = (s32[4,12]{1,0:T(4,128)S(1)}, s32[4,12]{1,0:T(4,128)}, u32[]{:S(2)}) copy-start(s32[4,12]{1,0:T(4,128)} %param.11) | copy-start | bytes 580
  16.7 77.0 %copy-start.19 = (s32[4]{0:T(128)S(1)}, s32[4]{0:T(128)}, u32[]{:S(2)}) copy-start(s32[4]{0:T(128)} %param.12) | copy-start | bytes 52
  18.0 191.0 %all-gather.8.cloned.1.call-start = ((), (), s32[]{:S(2)}) async-start(), calls=%async_computation.2 | async-start | bytes 17039360 | tf_op jit(solution)/shard_map/all_gather | solution.py:159
  230.2 0.8 copy-start.15
  232.4 3.9 %copy-start.12 = (f32[4,4]{1,0:T(4,128)S(1)}, f32[4,4]{1,0:T(4,128)}, u32[]{:S(2)}) copy-start(f32[4,4]{1,0:T(4,128)} %add_rsqrt_fusion) | copy-start | bytes 196
  232.5 4.8 %copy-start.2 = (f32[4,4,2048]{2,1,0:T(4,128)S(1)}, f32[4,4,2048]{2,1,0:T(4,128)}, u32[]{:S(2)}) copy-start(f32[4,4,2048]{2,1,0:T(4,128)} %constant_dynamic-slice_fusion) | copy-start | bytes 393220
  232.5 4.8 %copy-start.4 = (bf16[2,64,128]{2,1,0:T(8,128)(2,1)S(1)}, bf16[2,64,128]{2,1,0:T(8,128)(2,1)}, u32[]{:S(2)}) copy-start(bf16[2,64,128]{2,1,0:T(8,128)(2,1)} %param.17) | copy-start | bytes 98308
  232.5 5.0 %copy-start.6 = (f32[4,4,64]{2,1,0:T(4,128)S(1)}, f32[4,4,64]{2,1,0:T(4,128)}, u32[]{:S(2)}) copy-start(f32[4,4,64]{2,1,0:T(4,128)} %get-tuple-element.40) | copy-start | bytes 12292
  232.5 5.3 %copy-start.16 = (pred[4,4]{1,0:T(4,128)(4,1)S(1)}, pred[4,4]{1,0:T(4,128)(4,1)}, u32[]{:S(2)}) copy-start(pred[4,4]{1,0:T(4,128)(4,1)} %fusion.75) | copy-start | bytes 52
  232.5 23.5 %all-to-all-start = ((bf16[4,192,8,128]{3,1,0,2:T(8,128)(2,1)}), bf16[4,192,8,128]{3,1,0,2:T(8,128)(2,1)S(1)}, u32[]{:S(2)}, u32[]{:S(2)}) async-start(bf16[4,192,8,128]{3,1,0,2:T(8,128)(2,1)} %copy_select_fusion), calls=%async_computation | async-start | bytes 3145728 | tf_op jit(solution)/shard_map/all_to_all | solution.py:167
  237.7 18.2 %copy-start.7 = (bf16[4,4,2,8,64]{4,3,2,1,0:T(8,128)(2,1)}, bf16[4,4,2,8,64]{4,3,2,1,0:T(8,128)(2,1)S(1)}, u32[]{:S(2)}) copy-start(bf16[4,4,2,8,64]{4,3,2,1,0:T(8,128)(2,1)S(1)} %get-tuple-element.33) | copy-start | bytes 98308
  237.7 18.2 %copy-start.9 = (bf16[4,4,2,8,64]{4,3,2,1,0:T(8,128)(2,1)}, bf16[4,4,2,8,64]{4,3,2,1,0:T(8,128)(2,1)S(1)}, u32[]{:S(2)}) copy-start(bf16[4,4,2,8,64]{4,3,2,1,0:T(8,128)(2,1)S(1)} %get-tuple-element.34) | copy-start | bytes 98308
  256.0 0.8 copy-start.5
  257.3 0.8 copy-start.8
  257.3 0.9 copy-start.10
  257.3 0.9 copy-start.14
  258.2 0.7 copy-start.13
  258.2 0.9 copy-start.3
  258.2 0.9 copy-start.17
  258.2 1.5 copy-start.11
  286.2 10.0 %copy-start.1 = (bf16[128,8192]{1,0:T(8,128)(2,1)S(1)}, bf16[128,8192]{1,0:T(8,128)(2,1)}, u32[]{:S(2)}) copy-start(bf16[128,8192]{1,0:T(8,128)(2,1)} %param.15) | copy-start | bytes 6291460
Sparse Core Ops, SparseCore 0:
  18.1 189.1 all-reduce.2
Sparse Core Ops, SparseCore 1:
  21.7 109.0 all-gather.7
where the time goes:
time: 304 us
  waiting for transfers between devices  128 us (42%)
  blocking collectives  103 us (34%)
  matrix products  26.6 us (9%)
  local copies, waits for them, and re-layouts  16.5 us (5%)
  between operations  15.3 us (5%)
  other arithmetic  9.84 us (3%)
  starting transfers between devices  3.93 us (1%)
    psum x1, waiting for transfers between devices, local(): lax.psum((query_part, latent_part, square_part), SIDE_SEQ_HEAD)  111 us
    psum x1, blocking collectives, local(): lax.psum((query_part, latent_part, square_part), SIDE_SEQ_HEAD)  72.1 us
    all_gather x3, blocking collectives, all_in_one(): both, at, found = (lax.all_gather(jnp.concatenate(lines), axis), 0, {})  23.8 us
    dot_general x1, matrix products, local(): jnp.dot(token_rows, lax.all_gather(down_proj, SEQ_HEAD, axis=0, tiled=Tru...  18.7 us
    all_to_all x1, waiting for transfers between devices, local(): lax.all_to_all(ordered, 'head', split_axis=2, concat_axis=1, tiled=True)  16.5 us
    all_to_all x1, blocking collectives, sent_to_all(): lax.all_to_all(jnp.broadcast_to(array[None], (devices, *array.shape)), ax...  7.23 us
  transfers between devices with their start and end apart: 3, of which 2 were waited for; matrix products, arithmetic and copies ran while one was open for 3% of the time, Pallas kernels for 0%

commit v1 on v0

v1 whole, which is shorter than its diff:
```python
import functools
import math

import jax
import jax.numpy as jnp
from jax import lax
from jax.experimental import pallas as pl
from jax.experimental.pallas import tpu as pltpu
from jax.sharding import Mesh
from jax.sharding import PartitionSpec as P

D = 8192
HD = 128
PAGE = 16
SEQ = ("seq_0", "seq_1", "seq_2")
SIDE_SEQ_HEAD = ("side", "seq_0", "seq_1", "seq_2", "head")
SEQ_HEAD = ("seq_0", "seq_1", "seq_2", "head")
AXES = ("side", "seq_0", "seq_1", "seq_2", "head")
MESH = pl.DeviceIdType.MESH
rope_base = 500000.0
masked_score = -1e30
BF = jnp.bfloat16
F32 = jnp.float32


def pick_kernel(ids_ref, emb_ref, out_ref, blocks, rows, sems):
    vocab = emb_ref.shape[0]
    first = lax.axis_index("side") * vocab
    count = blocks.shape[0]
    width = ids_ref.shape[1]
    subs = []
    copies = []
    for i in range(count):
        raw = ids_ref[i // width, i % width] - first
        inside = jnp.logical_and(raw >= 0, raw < vocab)
        local = jnp.clip(raw, 0, vocab - 1)
        block = local // 16
        subs.append(jnp.where(inside, local - block * 16, -1))
        copy = pltpu.make_async_copy(
            emb_ref.at[pl.ds(pl.multiple_of(block * 16, 16), 16)], blocks.at[i], sems.at[i]
        )
        copy.start()
        copies.append(copy)
    line = lax.broadcasted_iota(jnp.int32, (16, HD), 0)
    for i in range(count):
        copies[i].wait()
        part = jnp.where(line == subs[i], blocks[i].astype(F32), 0.0)
        rows[pl.ds(i, 1), :] = jnp.sum(part, axis=0, keepdims=True)
    out_ref[...] = rows[...].astype(BF)


def pick(new_ids, embedding):
    count = new_ids.size
    return pl.pallas_call(
        pick_kernel,
        out_shape=jax.ShapeDtypeStruct((count, HD), BF),
        in_specs=[
            pl.BlockSpec(memory_space=pltpu.SMEM),
            pl.BlockSpec(memory_space=pl.ANY),
        ],
        out_specs=pl.BlockSpec(memory_space=pltpu.VMEM),
        scratch_shapes=[
            pltpu.VMEM((count, 16, HD), BF),
            pltpu.VMEM((count, HD), F32),
            pltpu.SemaphoreType.DMA((count,)),
        ],
        name="pick_rows",
    )(new_ids, embedding)


def rope(values, cosine, sine):
    return values * cosine + pltpu.roll(values, HD // 2, 1) * sine


def split_scalar(column):
    lane = lax.broadcasted_iota(jnp.int32, (column.shape[0], HD), 1)
    wide = jnp.broadcast_to(column, lane.shape)
    high = wide.astype(BF).astype(F32)
    middle = (wide - high).astype(BF).astype(F32)
    low = wide - high - middle
    return jnp.where(lane == 0, high, jnp.where(lane == 1, middle, low)).astype(BF)


def joined_scalar(block):
    part = block[:, HD:].astype(F32)
    return part[:, 0:1] + part[:, 1:2] + part[:, 2:3]


def merged(blocks):
    levels = [joined_scalar(b) for b in blocks]
    peak = functools.reduce(jnp.maximum, levels)
    weights = [jnp.exp(level - peak) for level in levels]
    total = functools.reduce(jnp.add, weights)
    summed = functools.reduce(
        jnp.add, [w * b[:, :HD].astype(F32) for w, b in zip(weights, blocks)]
    )
    return summed / total, peak + jnp.log(total)


STEPS = (
    (0, 0), (1, 0), (0, 1), (2, 0), (0, 2), (3, 0), (1, 1), (1, 2),
    (0, 3), (1, 3), (2, 1), (2, 2), (2, 3), (3, 1), (3, 2), (3, 3),
)
PART1 = (0, 4, 8, 12)
PART2 = (2, 6, 10, 13)


def pick_int(n, values):
    found = jnp.int32(values[0])
    for j in range(1, len(values)):
        found = jnp.where(n == j, jnp.int32(values[j]), found)
    return found


def offset_of(k):
    return k // 2 + 3 * (k % 2) - 2 * (k // 3)


def main_kernel(
    hid, down, picked, qproj, kv, outp, tab, bias_a, bias_b, ftab,
    out_ref,
    H, W, acc, QP, OP, kvb, ptab, pbias, pickb, part, rcore, qsum, rz, ry, rx, qz,
    Bm, FK, FV, Q, ob, cz, cmine, cy, cmine2, cx, ctx, fin,
    lsem, wl, hs, hr, ws, wr, xs, ps, pr, fs, fr, es, er,
):
    s, y, x, c, z = [lax.axis_index(a) for a in AXES]
    o = 1 - c

    def dev(s_=s, y_=y, x_=x, c_=c, z_=z):
        return (s_, y_, x_, c_, z_)

    core_dev = dev(c_=o)
    pair_dev = dev(s_=1 - s)
    cross_dev = dev(s_=1 - s, x_=1 - x)
    xhi_dev = dev(x_=1 - x)
    z_dev = [dev(z_=lax.rem(z + d, 4)) for d in (1, 2, 3)]
    y_dev = [dev(y_=lax.rem(y + d, 4)) for d in (1, 2, 3)]

    def remote(src, dst, send, recv, device):
        return pltpu.make_async_remote_copy(
            src_ref=src, dst_ref=dst, send_sem=send, recv_sem=recv,
            device_id=device, device_id_type=MESH,
        )

    qcopy = pltpu.make_async_copy(qproj, QP, lsem.at[4])
    qcopy.start()

    def ychunk(q):
        yy = lax.rem(y + (0, 3, 1, 2)[q], 4)
        return pl.ds(pl.multiple_of(yy * 2048, 2048), 2048)

    hlocal = [
        pltpu.make_async_copy(hid.at[:, ychunk(q)], H.at[0, :, ychunk(q)], lsem.at[q])
        for q in range(4)
    ]
    for copy in hlocal:
        copy.start()
    ocopy = pltpu.make_async_copy(outp, OP, lsem.at[5])
    ocopy.start()

    everyone = [core_dev, pair_dev, cross_dev, xhi_dev] + z_dev + y_dev
    barrier = pltpu.get_barrier_semaphore()
    for device in everyone:
        pl.semaphore_signal(barrier, inc=1, device_id=device, device_id_type=MESH)
    pl.semaphore_wait(barrier, len(everyone))

    sent = []

    def go(copy):
        copy.start()
        sent.append(copy)
        return copy

    ex = [0]

    def message(src, dst, device):
        k = ex[0]
        ex[0] += 1
        return remote(src, dst, es.at[k], er.at[k], device)

    m_pick = go(message(picked, pickb, pair_dev))
    own_rows = pl.ds(pl.multiple_of(c * 128, 128), 128)
    w_local = []
    w_init = []
    for i in range(4):
        theirs = pl.ds(pl.multiple_of((2 * i + o) * 128, 128), 128)
        w_init.append(go(remote(
            down.at[:, theirs], W.at[x, y, z, own_rows, pl.ds(i * 128, 128)],
            ws.at[i], wr.at[i], core_dev,
        )))
    for i in range(4):
        mine = pl.ds(pl.multiple_of((2 * i + c) * 128, 128), 128)
        copy = pltpu.make_async_copy(
            down.at[:, mine], W.at[x, y, z, own_rows, pl.ds(i * 128, 128)], wl.at[i]
        )
        copy.start()
        w_local.append(copy)
    hremote = [
        remote(hid.at[:, ychunk(q)], H.at[1, :, ychunk(q)], hs.at[q], hr.at[q], core_dev)
        for q in range(4)
    ]
    go(hremote[0])
    m_kv = [go(message(kv.at[c], kvb.at[z], z_dev[d])) for d in range(3)]

    in_plane = pl.ds(pl.multiple_of(s * 64, 64), 192)
    prow = pl.ds(pl.multiple_of(s * 224, 32), 32)
    crow = pl.ds(pl.multiple_of(32 + s * 160, 32), 32)
    ia = z * o + y * c
    ib = y * o + z * c

    def place(a_off, b_off):
        a_at = lax.rem(ia + a_off, 4)
        b_at = lax.rem(ib + b_off, 4)
        return (b_at * o + a_at * c, a_at * o + b_at * c)

    def unit(u):
        return x + u - 2 * x * u

    def a_dev(step):
        return dev(y_=lax.rem(y + step * c, 4), z_=lax.rem(z + step * o, 4))

    def b_dev(step):
        return dev(y_=lax.rem(y + step * o, 4), z_=lax.rem(z + step * c, 4))

    def piece(line, m, along_a, a_off):
        u = (0, 1, 0, 1, 0, 1)[m]
        step = (1, 1, 3, 3, 1, 3)[m]
        off = (0, 0, 0, 0, 3, 1)[m]
        if along_a:
            at = place(off, 0)
            device = a_dev(step)
        else:
            at = place(a_off, off)
            device = b_dev(step)
        ref = W.at[unit(u), at[0], at[1], in_plane]
        return remote(ref, ref, ps.at[line, m], pr.at[line, m], device)

    def a_piece(m):
        return piece(4, m, True, None)

    def b_piece(k, m):
        return piece(k, m, False, offset_of(k))

    def side_piece(k, b, which):
        at = place(offset_of(k), offset_of(b))
        rows = prow if which == 0 else crow
        ref = W.at[:, at[0], at[1], rows]
        return remote(
            ref, ref, fs.at[k, b, which], fr.at[k, b, which], pair_dev if which == 0 else cross_dev
        )

    def side_start(k, b):
        side_piece(k, b, 0).start()
        side_piece(k, b, 1).start()

    for copy in w_local:
        copy.wait()
    for copy in w_init:
        copy.wait_recv()
    own = W.at[x, y, z]
    m_cross = go(remote(own, own, xs.at[0], xs.at[1], cross_dev))
    for m in (0, 2):
        a_piece(m).start()
        b_piece(0, m).start()

    m_pick.wait_recv()
    both = (picked[...].astype(F32) + pickb[...].astype(F32)).astype(BF)
    pickb[...] = both
    rows16 = pickb[pl.ds(pl.multiple_of(s * 16, 16), 16), :]
    wide16 = rows16.astype(F32)
    squares = wide16 * wide16
    qcopy.wait()
    for cc in (0, 1):
        for i in range(4):
            g = 2 * i + cc
            part[cc, i, :, 0:1024] = jnp.dot(
                rows16, QP[:, g * 1024 : (g + 1) * 1024], preferred_element_type=F32
            )
            part[cc, i, :, 1024:1152] = jnp.dot(
                rows16, down[:, g * 128 : (g + 1) * 128], preferred_element_type=F32
            )
            part[cc, i, :, 1152:1280] = squares
    m_core = go(message(part.at[o], rcore, core_dev))
    m_tab = go(message(tab, ptab, core_dev))
    m_bias = go(message(bias_b, pbias, core_dev))
    for q in (1, 2, 3):
        go(hremote[q])

    m_cross.wait_recv()
    for m in (1, 3):
        a_piece(m).start()
        b_piece(0, m).start()

    a_piece(0).wait_recv()
    a_piece(4).start()
    b_piece(1, 0).start()
    b_piece(1, 2).start()
    a_piece(2).wait_recv()
    b_piece(2, 0).start()
    b_piece(2, 2).start()

    m_core.wait_recv()
    for i in range(4):
        qsum[i] = part[c, i] + rcore[i]
    m_z = [
        go(message(qsum.at[lax.rem(z + d, 4)], rz.at[d - 1], z_dev[d - 1])) for d in (1, 2, 3)
    ]

    a_piece(1).wait_recv()
    b_piece(1, 1).start()
    b_piece(1, 3).start()
    side_start(1, 0)
    a_piece(3).wait_recv()
    a_piece(5).start()
    b_piece(2, 1).start()
    b_piece(2, 3).start()
    side_start(2, 0)

    for m in m_z:
        m.wait_recv()
    rz[3] = qsum[z] + rz[0] + rz[1] + rz[2]
    m_y = [go(message(rz.at[3], ry.at[d - 1], y_dev[d - 1])) for d in (1, 2, 3)]

    a_piece(4).wait_recv()
    b_piece(3, 0).start()
    b_piece(3, 2).start()
    a_piece(5).wait_recv()
    b_piece(3, 1).start()
    b_piece(3, 3).start()
    side_start(3, 0)

    for m in m_y:
        m.wait_recv()
    ry[3] = rz[3] + ry[0] + ry[1] + ry[2]
    m_x = go(message(ry.at[3], rx, xhi_dev))

    lines = [st[0] for st in STEPS]
    places = [st[1] for st in STEPS]

    m_q = [message(qz.at[z], qz.at[z], z_dev[d - 1]) for d in (1, 2, 3)]
    sent.extend(m_q)

    def step(n, carry):
        for k in range(4):
            @pl.when(n == PART1[k])
            def _():
                b_piece(k, 0).wait_recv()
                b_piece(k, 4).start()
                b_piece(k, 3).wait_recv()
                b_piece(k, 5).start()
                b_piece(k, 1).wait_recv()
                side_start(k, 1)
                b_piece(k, 2).wait_recv()
                side_start(k, 2)

            @pl.when(n == PART2[k])
            def _():
                b_piece(k, 4).wait_recv()
                b_piece(k, 5).wait_recv()
                side_start(k, 3)

        @pl.when(n == 1)
        def _():
            m_x.wait_recv()
            total = ry[3] + rx[...]
            inverse = lax.rsqrt(
                jnp.sum(total[:, 1152:1280], axis=1, keepdims=True) / D + 1e-05
            )
            cosine = ftab[:, 0:128]
            sine = ftab[:, 128:256]
            for j in range(8):
                head = total[:, j * 128 : (j + 1) * 128] * inverse
                qz[z, :, j * 128 : (j + 1) * 128] = rope(head, cosine, sine).astype(BF)
            qz[z, :, 1024:1152] = (total[:, 1024:1152] * inverse).astype(BF)
            for m in m_q:
                m.start()

        for q, at in enumerate((0, 1, 3, 5)):
            @pl.when(n == at)
            def _():
                hlocal[q].wait()
                hremote[q].wait_recv()

        k = pick_int(n, lines)
        b = pick_int(n, places)

        @pl.when(n > 0)
        def _():
            side_piece(k, b, 0).wait_recv()
            side_piece(k, b, 1).wait_recv()

        yy, zz = place(offset_of(k), offset_of(b))

        def columns(xh, core):
            return pl.ds(pl.multiple_of((((yy * 2 + xh) * 2 + core) * 4 + zz) * 128, 128), 128)

        def tile(m, carry):
            t = m // 2
            rows = pl.ds(pl.multiple_of((m % 2) * 384, 384), 384)
            left = [
                jnp.concatenate([H[t, rows, columns(xh, 0)], H[t, rows, columns(xh, 1)]], axis=1)
                for xh in (0, 1)
            ]
            product = jnp.dot(left[0], W[0, yy, zz], preferred_element_type=F32) + jnp.dot(
                left[1], W[1, yy, zz], preferred_element_type=F32
            )

            @pl.when(n == 0)
            def _():
                acc[t, rows, :] = product

            @pl.when(n > 0)
            def _():
                acc[t, rows, :] += product

            return carry

        lax.fori_loop(0, 4, tile, 0)
        return carry

    lax.fori_loop(0, 16, step, 0)

    for m in m_kv:
        m.wait_recv()
    kvb[z] = kv[c]
    for m in m_q:
        m.wait_recv()
    m_tab.wait_recv()
    m_bias.wait_recv()
    pbias[...] = pbias[...] + bias_a[...]
    line = lax.broadcasted_iota(jnp.int32, (128, 128), 0)
    lane = lax.broadcasted_iota(jnp.int32, (128, 128), 1)
    to_requests = (
        lane == (line % 32) // 4 * 16 + line // 32 * 4 + line % 4
    ).astype(F32).astype(BF)
    to_heads = (
        lane == (line % 16) // 4 * 32 + line // 16 * 4 + line % 4
    ).astype(F32).astype(BF)
    for i in range(4):
        weights = kvb[i]
        zero = jnp.zeros_like(weights)
        Bm[i, :, 0:128] = jnp.where(line < 64, weights, zero)
        Bm[i, :, 128:256] = jnp.where(line < 64, zero, weights)
        heads = jnp.concatenate([qz[i, :, j * 128 : (j + 1) * 128] for j in range(8)], axis=0)
        Q[i] = jnp.dot(to_requests, heads, preferred_element_type=F32).astype(BF)
        fresh = jnp.dot(qz[i, :, 1024:1152], Bm[i], preferred_element_type=F32)
        pad = jnp.zeros((112, 128), BF)
        FK[i] = jnp.concatenate(
            [rope(fresh[:, 0:128], ftab[:, 0:128], ftab[:, 128:256]).astype(BF), pad], axis=0
        )
        FV[i] = jnp.concatenate([fresh[:, 128:256].astype(BF), pad], axis=0)

    elsewhere = jnp.where((y + x + z) == 0, 0.0, masked_score)
    row32 = lax.broadcasted_iota(jnp.int32, (32, 128), 0)
    col32 = lax.broadcasted_iota(jnp.int32, (32, 128), 1)
    scaling = 1.0 / math.sqrt(HD)

    def request(r, carry):
        rows = pl.ds(pl.multiple_of(r * 192, 64), 192)
        cosine = jnp.concatenate([tab[rows, 0:128], ptab[rows, 0:128]], axis=0)
        sine = jnp.concatenate([tab[rows, 128:256], ptab[rows, 128:256]], axis=0)
        seen = (col32 // 4 == r) & (col32 % 4 <= row32 % 4)
        mask = jnp.concatenate(
            [
                jnp.broadcast_to(pbias[pl.ds(r, 1), :], (32, 384)),
                jnp.where(seen, elsewhere, masked_score),
            ],
            axis=1,
        )
        for i in range(4):
            latent = jnp.concatenate(
                [acc[0, rows, i * 128 : (i + 1) * 128], acc[1, rows, i * 128 : (i + 1) * 128]],
                axis=0,
            ).astype(BF)
            rebuilt = jnp.dot(latent, Bm[i], preferred_element_type=F32)
            keys = jnp.concatenate(
                [rope(rebuilt[:, 0:128], cosine, sine).astype(BF), FK[i]], axis=0
            )
            values = jnp.concatenate([rebuilt[:, 128:256].astype(BF), FV[i]], axis=0)
            query = Q[i, pl.ds(pl.multiple_of(r * 32, 32), 32), :]
            scores = lax.dot_general(
                query, keys, (((1,), (1,)), ((), ())), preferred_element_type=F32
            ) * scaling + mask
            peak = jnp.max(scores, axis=1, keepdims=True)
            e = jnp.where(mask > -1e29, jnp.exp(scores - peak), 0.0)
            total = jnp.sum(e, axis=1, keepdims=True)
            context = jnp.dot(e.astype(BF), values, preferred_element_type=F32)
            some = total > 0.0
            safe = jnp.where(some, total, 1.0)
            level = jnp.where(some, peak + jnp.log(safe), masked_score)
            at = pl.ds(pl.multiple_of(r * 32, 32), 32)
            ob[i, at, 0:128] = (context / safe).astype(BF)
            ob[i, at, 128:256] = split_scalar(level)
        return carry

    lax.fori_loop(0, 4, request, 0)

    m_cz = [
        go(message(ob.at[lax.rem(z + d, 4)], cz.at[d - 1], z_dev[d - 1])) for d in (1, 2, 3)
    ]
    for m in m_cz:
        m.wait_recv()
    value, level = merged([ob[z], cz[0], cz[1], cz[2]])
    cmine[:, 0:128] = value.astype(BF)
    cmine[:, 128:256] = split_scalar(level)
    m_cy = [go(message(cmine, cy.at[d - 1], y_dev[d - 1])) for d in (1, 2, 3)]
    for m in m_cy:
        m.wait_recv()
    value, level = merged([cmine[...], cy[0], cy[1], cy[2]])
    cmine2[:, 0:128] = value.astype(BF)
    cmine2[:, 128:256] = split_scalar(level)
    m_cx = go(message(cmine2, cx, xhi_dev))
    m_cx.wait_recv()
    value, _ = merged([cmine2[...], cx[...]])
    ctx[c] = jnp.dot(to_heads, value.astype(BF), preferred_element_type=F32).astype(BF)
    m_ctx = go(message(ctx.at[c], ctx.at[c], core_dev))
    m_ctx.wait_recv()
    ocopy.wait()
    left = jnp.concatenate(
        [ctx[g, j * 16 : (j + 1) * 16, :] for g in range(2) for j in range(8)], axis=1
    )
    fin[z] = jnp.dot(left, OP[...], preferred_element_type=F32)
    m_fin = [go(message(fin.at[z], fin.at[z], z_dev[d - 1])) for d in (1, 2, 3)]
    for m in m_fin:
        m.wait_recv()
    out_ref[...] = (fin[0] + fin[1] + fin[2] + fin[3]).astype(BF)

    for copy in sent:
        copy.wait_send()
    for m in range(6):
        a_piece(m).wait_send()

    def drain(k, carry):
        for m in range(6):
            b_piece(k, m).wait_send()
        for b in range(4):
            @pl.when(k + b > 0)
            def _():
                side_piece(k, b, 0).wait_send()
                side_piece(k, b, 1).wait_send()
        return carry

    lax.fori_loop(0, 4, drain, 0)


MESSAGES = 1 + 3 + 3 + 3 + 3 + 1 + 3 + 3 + 3 + 1 + 1 + 3


def main(hid, down, picked, qproj, kv, outp, tab, bias_a, bias_b, ftab):
    vm = pl.BlockSpec(memory_space=pltpu.VMEM)
    anyspace = pl.BlockSpec(memory_space=pl.ANY)
    V = pltpu.VMEM
    S = pltpu.SemaphoreType.DMA
    return pl.pallas_call(
        main_kernel,
        out_shape=jax.ShapeDtypeStruct((16, 512), BF),
        in_specs=[anyspace, vm, vm, anyspace, vm, anyspace, vm, vm, vm, vm],
        out_specs=vm,
        scratch_shapes=[
            V((2, 768, 8192), BF),
            V((2, 4, 4, 256, 512), BF),
            V((2, 768, 512), F32),
            V((128, 8192), BF),
            V((2048, 512), BF),
            V((4, 128, 128), BF),
            V((768, 256), F32),
            V((8, 384), F32),
            V((32, 128), BF),
            V((2, 4, 16, 1280), F32),
            V((4, 16, 1280), F32),
            V((4, 16, 1280), F32),
            V((4, 16, 1280), F32),
            V((4, 16, 1280), F32),
            V((16, 1280), F32),
            V((4, 16, 1152), BF),
            V((4, 128, 256), BF),
            V((4, 128, 128), BF),
            V((4, 128, 128), BF),
            V((4, 128, 128), BF),
            V((4, 128, 256), BF),
            V((3, 128, 256), BF),
            V((128, 256), BF),
            V((3, 128, 256), BF),
            V((128, 256), BF),
            V((128, 256), BF),
            V((2, 128, 128), BF),
            V((4, 16, 512), F32),
            S((6,)),
            S((4,)),
            S((4,)),
            S((4,)),
            S((4,)),
            S((4,)),
            S((2,)),
            S((5, 6)),
            S((5, 6)),
            S((4, 4, 2)),
            S((4, 4, 2)),
            S((MESSAGES,)),
            S((MESSAGES,)),
        ],
        compiler_params=pltpu.CompilerParams(
            collective_id=0, has_side_effects=True, vmem_limit_bytes=62 * 2**20
        ),
        name="gather_decode",
    )(hid, down, picked, qproj, kv, outp, tab, bias_a, bias_b, ftab)


def rope_table(positions):
    half = HD // 2
    frequency = 1.0 / rope_base ** (jnp.arange(half, dtype=F32) * 2.0 / HD)
    angles = positions.astype(F32)[:, None] * frequency
    cosine = jnp.cos(angles)
    sine = jnp.sin(angles)
    return jnp.concatenate([cosine, cosine, -sine, sine], axis=1)


def local(
    cached_hidden, page_order, lengths, new_ids, embedding,
    query_proj, down_proj, key_up, value_up, out_proj,
):
    requests, span, width = cached_hidden.shape
    steps = new_ids.shape[1]
    pages = span // PAGE
    picked = pick(new_ids, embedding)
    run = lax.axis_index(SEQ_HEAD)
    slots = jnp.arange(pages, dtype=jnp.int32)
    logical = jnp.sum(
        jnp.where(page_order[:, None, :] == slots[None, :, None], slots[None, None, :], 0), axis=2
    )
    positions = (
        run * span + logical[:, :, None] * PAGE + jnp.arange(PAGE, dtype=jnp.int32)[None, None, :]
    ).reshape(requests, span)
    tab = rope_table(positions.reshape(-1))
    bias = jnp.where(positions < lengths[:, None], 0.0, masked_score).astype(F32)
    bias_a = jnp.pad(bias, ((0, 4), (0, span)))
    bias_b = jnp.pad(bias, ((0, 4), (span, 0)))
    fresh = (lengths[:, None] + jnp.arange(steps, dtype=jnp.int32)[None, :]).reshape(-1)
    ftab = rope_table(fresh)
    kv = jnp.concatenate([key_up, value_up], axis=1)
    out = main(
        cached_hidden.reshape(requests * span, width), down_proj, picked, query_proj, kv,
        out_proj, tab, bias_a, bias_b, ftab,
    )
    return out.reshape(requests, steps, -1)


def solution(mesh):
    finer = Mesh(
        mesh.devices.reshape(mesh.shape["side"], 4, 2, 2, mesh.shape["head"]), AXES
    )
    placed = (
        P("side", SEQ_HEAD, None),
        P("side", SEQ_HEAD),
        P("side"),
        P(),
        P("side", SEQ_HEAD),
        P(SEQ_HEAD, None),
        P(SEQ_HEAD, None),
        P("head", None, None),
        P("head", None, None),
        P("head", SEQ),
    )
    return jax.shard_map(
        local, mesh=finer, in_specs=placed, out_specs=P("side", None, SEQ), check_vma=False
    )
```

time: 304 us -> 123 us (0.40)
  waiting for transfers between devices: 128 us -> 0 us
  Pallas kernels: 0 us -> 111 us
  blocking collectives: 103 us -> 0 us
  matrix products: 26.6 us -> 0 us
  between operations: 15.3 us -> 0.05 us
  local copies, waits for them, and re-layouts: 16.5 us -> 3.86 us
  starting transfers between devices: 3.93 us -> 0 us
    pallas_call x0 -> x2, Pallas kernels: none -> 111 us  [the longest x1 109 us: main(): pl.pallas_call(main_kernel, out_shape=jax.ShapeDtypeStruct((16, 512), BF)...]
    psum x1 -> x0, waiting for transfers between devices: 111 us -> none  [local(): lax.psum((query_part, latent_part, square_part), SIDE_SEQ_HEAD)]
    psum x1 -> x0, blocking collectives: 72.1 us -> none  [local(): lax.psum((query_part, latent_part, square_part), SIDE_SEQ_HEAD)]
    dot_general x10 -> x0, matrix products: 26.6 us -> none  [the longest x1 18.7 us: local(): jnp.dot(token_rows, lax.all_gather(down_proj, SEQ_HEAD, axis=0, tiled=Tru...]
    all_gather x3 -> x0, blocking collectives: 23.8 us -> none  [all_in_one(): both, at, found = (lax.all_gather(jnp.concatenate(lines), axis), 0, {})]
    all_to_all x1 -> x0, waiting for transfers between devices: 16.5 us -> none  [local(): lax.all_to_all(ordered, 'head', split_axis=2, concat_axis=1, tiled=True)]
    gather x3 -> x0, local copies, waits for them, and re-layouts: 7.43 us -> none  [the longest x1 4.99 us: local(): picked = jnp.take(embedding, jnp.clip(local_ids, 0, vocab_half - 1), axis=0)]
    all_to_all x1 -> x0, blocking collectives: 7.23 us -> none  [sent_to_all(): lax.all_to_all(jnp.broadcast_to(array[None], (devices, *array.shape)), ax...]
  transfers between devices with their start and end apart: 3 -> 0, of which waited for: 2 -> 0; matrix products, arithmetic and copies ran while one was open for 3% -> 0% of each run, Pallas kernels for 0% -> 0%
where the time goes in v1:
time: 123 us
  Pallas kernels  111 us (90%)
  other arithmetic  7.43 us (6%)
  local copies, waits for them, and re-layouts  3.86 us (3%)
    pallas_call x1, Pallas kernels, main(): pl.pallas_call(main_kernel, out_shape=jax.ShapeDtypeStruct((16, 512), BF)...  109 us
    pallas_call x1, Pallas kernels, pick(): pl.pallas_call(pick_kernel, out_shape=jax.ShapeDtypeStruct((count, HD), B...  2.8 us

profile of v1, /device:TPU:1, one launch (start us, length us, event | category | flops | bytes accessed | tf_op | source)
XLA Modules:
  0.0 122.7 jit_solution(10039921394458023309)
XLA Ops:
  0.0 1.0 select_reduce_fusion
  1.0 0.1 copy.16
  1.1 0.1 add_convert_fusion
  1.1 0.1 convert_element_type.25
  1.2 1.5 %multiply_cosine_fusion = (f32[768,64]{1,0:T(8,128)S(1)}, f32[768,64]{1,0:T(8,128)S(1)}, f32[768,64]{1,0:T(8,128)S(1)}) fusion(f32[768]{0:T(1024)S(1)} %convert_element_type.25, f32[64]{0:T(128)S(1)} %negate_power_fusion), kind=kLoop, calls=%fused_computation.2 | loop fusion | flops 98304 | bytes 593152 | tf_op jit(solution)/shard_map/cos | solution.py:613
  2.7 1.3 %pad_maximum_fusion.tab = f32[768,256]{1,0:T(8,128)} fusion(f32[768,64]{1,0:T(8,128)S(1)} %get-tuple-element.7, f32[768,64]{1,0:T(8,128)S(1)} %get-tuple-element.6, f32[768,64]{1,0:T(8,128)S(1)} %get-tuple-element.5), kind=kLoop, calls=%fused_computation | loop fusion | flops 589824 | bytes 1376256 | tf_op jit(solution)/shard_map/concatenate | solution.py:615
  4.0 0.1 add.78
  4.0 0.1 add.81
  4.1 0.1 add.83
  4.2 0.7 fusion.1
  4.9 0.7 fusion.3
  5.6 0.7 add_convert_fusion.1
  6.3 0.1 convert_element_type.27
  6.4 0.1 multiply_cosine_fusion.1
  6.5 0.7 pad_maximum_fusion.2.ftab
  7.2 1.4 %pad_maximum_fusion.1.kv = bf16[2,128,128]{2,1,0:T(8,128)(2,1)} fusion(bf16[2,64,128]{2,1,0:T(8,128)(2,1)} %param.18, bf16[2,64,128]{2,1,0:T(8,128)(2,1)} %param.17), kind=kLoop, calls=%fused_computation.4 | loop fusion | flops 131072 | bytes 131072 | tf_op jit(solution)/shard_map/concatenate | solution.py:640
  8.6 1.3 %copy.15.ids_ref = s32[8,4]{1,0:T(8,128)} copy(s32[8,4]{0,1:T(4,128)} %param.13) | data formatting | bytes 256 | tf_op args[3]
  10.0 2.8 %pick_rows.1.picked = bf16[32,128]{1,0:T(8,128)(2,1)} custom-call(s32[8,4]{1,0:T(8,128)} %copy.15.ids_ref, bf16[32256,128]{1,0:T(8,128)(2,1)} %emb_ref.1), custom_call_target="tpu_custom_call" | custom-call | tf_op jit(solution)/shard_map/pick_rows/pallas_call | solution.py:54
  12.8 108.5 %gather_decode.1 = bf16[16,512]{1,0:T(8,128)(2,1)} custom-call(bf16[768,8192]{1,0:T(8,128)(2,1)} %bitcast.1, bf16[128,1024]{1,0:T(8,128)(2,1)} %down.1, bf16[32,128]{1,0:T(8,128)(2,1)} %pick_rows.1.picked, bf16[128,8192]{1,0:T(8,128)(2,1)} %qproj.1, bf16[2,128,128]{2,1,0:T(8,128)(2,1)} %pad_maximum_fusion.1.kv, bf16[2048,512]{1,0:T(8,128)(2,1)} %outp.1, ...), custom_call_target="tpu_custom_call" | custom-call | tf_op jit(solution)/shard_map/gather_decode/pallas_call | solution.py:554
  121.3 1.3 %reshape.53 = bf16[4,4,512]{2,1,0:T(4,128)(2,1)} reshape(bf16[16,512]{1,0:T(8,128)(2,1)} %gather_decode.1) | data formatting | bytes 32768 | tf_op jit(solution)/shard_map/reshape | solution.py:645
  (3 shorter events, 0.0 us)

commit v2 on v1

--- a/solution.py
+++ b/solution.py
@@ -3,6 +3,7 @@
 
 import jax
 import jax.numpy as jnp
+import numpy as np
 from jax import lax
 from jax.experimental import pallas as pl
 from jax.experimental.pallas import tpu as pltpu
@@ -23,15 +24,22 @@
 F32 = jnp.float32
 
 
-def pick_kernel(ids_ref, emb_ref, out_ref, blocks, rows, sems):
+def prepare_kernel(
+    ids_ref, order_ref, lengths_ref, freq_ref, emb_ref,
+    out_ref, page_ref, fresh_ref, bias_ref,
+    blocks, rows, line_at, sems,
+):
     vocab = emb_ref.shape[0]
     first = lax.axis_index("side") * vocab
     count = blocks.shape[0]
-    width = ids_ref.shape[1]
+    steps = ids_ref.shape[0]
+    requests, pages = order_ref.shape
+    span = pages * PAGE
+    start = lax.axis_index(SEQ_HEAD) * span
     subs = []
     copies = []
     for i in range(count):
-        raw = ids_ref[i // width, i % width] - first
+        raw = ids_ref[i % steps, i // steps] - first
         inside = jnp.logical_and(raw >= 0, raw < vocab)
         local = jnp.clip(raw, 0, vocab - 1)
         block = local // 16
@@ -41,6 +49,33 @@
         )
         copy.start()
         copies.append(copy)
+    lane = lax.broadcasted_iota(jnp.int32, (1, 384), 1)
+    bias_ref[...] = jnp.zeros_like(bias_ref)
+    for r in range(requests):
+        at = jnp.zeros((1, 384), jnp.int32)
+        for j in range(pages):
+            k = order_ref[r, j]
+            line_at[pl.ds(r * pages + k, 1), :] = jnp.full((1, HD), start + j * PAGE, jnp.int32)
+            at = jnp.where(
+                (lane // PAGE) % pages == k, start + j * PAGE + lane % PAGE, at
+            )
+        dead = jnp.where(at < lengths_ref[r], 0.0, masked_score)
+        bias_ref[0, pl.ds(r, 1), :] = jnp.where(lane < span, dead, 0.0)
+        bias_ref[1, pl.ds(r, 1), :] = jnp.where(lane >= span, dead, 0.0)
+        for t in range(steps):
+            line_at[pl.ds(requests * pages + r * steps + t, 1), :] = jnp.full(
+                (1, HD), lengths_ref[r] + t, jnp.int32
+            )
+    offset = lax.broadcasted_iota(jnp.int32, (PAGE, HD), 0)
+    line_at[pl.ds(64, PAGE), :] = offset
+    angles = line_at[...].astype(F32) * freq_ref[0:1, :]
+    cosine = jnp.cos(angles)
+    sine = jnp.sin(angles)
+    page_ref[:, 0:HD] = cosine
+    page_ref[:, HD : 2 * HD] = sine
+    half = lax.broadcasted_iota(jnp.int32, (16, HD), 1) < HD // 2
+    fresh_ref[:, 0:HD] = cosine[48:64]
+    fresh_ref[:, HD : 2 * HD] = jnp.where(half, -sine[48:64], sine[48:64])
     line = lax.broadcasted_iota(jnp.int32, (16, HD), 0)
     for i in range(count):
         copies[i].wait()
@@ -49,60 +84,74 @@
     out_ref[...] = rows[...].astype(BF)
 
 
-def pick(new_ids, embedding):
+def prepare(new_ids, page_order, lengths, freq, embedding):
     count = new_ids.size
+    smem = pl.BlockSpec(memory_space=pltpu.SMEM)
+    vm = pl.BlockSpec(memory_space=pltpu.VMEM)
     return pl.pallas_call(
-        pick_kernel,
-        out_shape=jax.ShapeDtypeStruct((count, HD), BF),
-        in_specs=[
-            pl.BlockSpec(memory_space=pltpu.SMEM),
-            pl.BlockSpec(memory_space=pl.ANY),
-        ],
-        out_specs=pl.BlockSpec(memory_space=pltpu.VMEM),
+        prepare_kernel,
+        out_shape=(
+            jax.ShapeDtypeStruct((count, HD), BF),
+            jax.ShapeDtypeStruct((80, 2 * HD), F32),
+            jax.ShapeDtypeStruct((16, 2 * HD), F32),
+            jax.ShapeDtypeStruct((2, 8, 384), F32),
+        ),
+        in_specs=[smem, smem, smem, vm, pl.BlockSpec(memory_space=pl.ANY)],
+        out_specs=(vm, vm, vm, vm),
         scratch_shapes=[
             pltpu.VMEM((count, 16, HD), BF),
             pltpu.VMEM((count, HD), F32),
+            pltpu.VMEM((80, HD), jnp.int32),
             pltpu.SemaphoreType.DMA((count,)),
         ],
-        name="pick_rows",
-    )(new_ids, embedding)
+        name="prepare",
+    )(new_ids.T, page_order, lengths, freq, embedding)
 
 
 def rope(values, cosine, sine):
     return values * cosine + pltpu.roll(values, HD // 2, 1) * sine
 
 
-def split_scalar(column):
+def coded(column):
     lane = lax.broadcasted_iota(jnp.int32, (column.shape[0], HD), 1)
     wide = jnp.broadcast_to(column, lane.shape)
     high = wide.astype(BF).astype(F32)
     middle = (wide - high).astype(BF).astype(F32)
     low = wide - high - middle
-    return jnp.where(lane == 0, high, jnp.where(lane == 1, middle, low)).astype(BF)
-
-
-def joined_scalar(block):
-    part = block[:, HD:].astype(F32)
-    return part[:, 0:1] + part[:, 1:2] + part[:, 2:3]
+    parts = jnp.where(lane == 0, high, jnp.where(lane == 1, middle, jnp.where(lane == 2, low, 0.0)))
+    line16 = lax.broadcasted_iota(jnp.int32, (16, HD), 0)
+    lane16 = lax.broadcasted_iota(jnp.int32, (16, HD), 1)
+    first = (line16 == lane16).astype(F32).astype(BF)
+    return lax.dot_general(
+        first, parts.astype(BF), (((1,), (1,)), ((), ())), preferred_element_type=F32
+    ).astype(BF)
+
+
+def decoded(rows):
+    line16 = lax.broadcasted_iota(jnp.int32, (16, HD), 0)
+    ones = jnp.where(line16 < 3, 1.0, 0.0).astype(BF)
+    return lax.dot_general(
+        rows, ones, (((0,), (0,)), ((), ())), preferred_element_type=F32
+    )
 
 
 def merged(blocks):
-    levels = [joined_scalar(b) for b in blocks]
+    levels = [decoded(b[128:144]) for b in blocks]
     peak = functools.reduce(jnp.maximum, levels)
     weights = [jnp.exp(level - peak) for level in levels]
     total = functools.reduce(jnp.add, weights)
     summed = functools.reduce(
-        jnp.add, [w * b[:, :HD].astype(F32) for w, b in zip(weights, blocks)]
+        jnp.add, [w * b[0:128].astype(F32) for w, b in zip(weights, blocks)]
     )
-    return summed / total, peak + jnp.log(total)
+    return summed / total, (peak + jnp.log(total))[:, 0:1]
 
 
 STEPS = (
-    (0, 0), (1, 0), (0, 1), (2, 0), (0, 2), (3, 0), (1, 1), (1, 2),
-    (0, 3), (1, 3), (2, 1), (2, 2), (2, 3), (3, 1), (3, 2), (3, 3),
+    (0, 0), (1, 0), (2, 0), (0, 1), (0, 2), (1, 1), (1, 2), (3, 0),
+    (2, 1), (2, 2), (3, 1), (3, 2), (0, 3), (1, 3), (2, 3), (3, 3),
 )
-PART1 = (0, 4, 8, 12)
-PART2 = (2, 6, 10, 13)
+PART1 = (1, 3, 5, 7)
+PART2 = (9, 10, 11, 12)
 
 
 def pick_int(n, values):
@@ -117,10 +166,10 @@
 
 
 def main_kernel(
-    hid, down, picked, qproj, kv, outp, tab, bias_a, bias_b, ftab,
+    hid, down, picked, qproj, ku, vu, outp, page, bias, ftab,
     out_ref,
-    H, W, acc, QP, OP, kvb, ptab, pbias, pickb, part, rcore, qsum, rz, ry, rx, qz,
-    Bm, FK, FV, Q, ob, cz, cmine, cy, cmine2, cx, ctx, fin,
+    H, W, acc, QP, OP, kub, vub, tabs, ppage, pbias, pickb, part, rcore, qsum, rz, ry, rx, qz,
+    Bm, FK, FV, Q, ob, lev, cz, cmine, cy, cx, fin,
     lsem, wl, hs, hr, ws, wr, xs, ps, pr, fs, fr, es, er,
 ):
     s, y, x, c, z = [lax.axis_index(a) for a in AXES]
@@ -142,23 +191,19 @@
             device_id=device, device_id_type=MESH,
         )
 
+    own_rows = pl.ds(pl.multiple_of(c * 128, 128), 128)
+    w_local = []
+    for i in range(4):
+        mine = pl.ds(pl.multiple_of((2 * i + c) * 128, 128), 128)
+        copy = pltpu.make_async_copy(
+            down.at[:, mine], W.at[x, y, z, own_rows, pl.ds(i * 128, 128)], wl.at[i]
+        )
+        copy.start()
+        w_local.append(copy)
     qcopy = pltpu.make_async_copy(qproj, QP, lsem.at[4])
     qcopy.start()
 
-    def ychunk(q):
-        yy = lax.rem(y + (0, 3, 1, 2)[q], 4)
-        return pl.ds(pl.multiple_of(yy * 2048, 2048), 2048)
-
-    hlocal = [
-        pltpu.make_async_copy(hid.at[:, ychunk(q)], H.at[0, :, ychunk(q)], lsem.at[q])
-        for q in range(4)
-    ]
-    for copy in hlocal:
-        copy.start()
-    ocopy = pltpu.make_async_copy(outp, OP, lsem.at[5])
-    ocopy.start()
-
-    everyone = [core_dev, pair_dev, cross_dev, xhi_dev] + z_dev + y_dev
+    everyone = [core_dev, pair_dev, cross_dev, xhi_dev, dev(x_=1 - x, c_=o)] + z_dev + y_dev
     barrier = pltpu.get_barrier_semaphore()
     for device in everyone:
         pl.semaphore_signal(barrier, inc=1, device_id=device, device_id_type=MESH)
@@ -179,8 +224,6 @@
         return remote(src, dst, es.at[k], er.at[k], device)
 
     m_pick = go(message(picked, pickb, pair_dev))
-    own_rows = pl.ds(pl.multiple_of(c * 128, 128), 128)
-    w_local = []
     w_init = []
     for i in range(4):
         theirs = pl.ds(pl.multiple_of((2 * i + o) * 128, 128), 128)
@@ -188,19 +231,22 @@
             down.at[:, theirs], W.at[x, y, z, own_rows, pl.ds(i * 128, 128)],
             ws.at[i], wr.at[i], core_dev,
         )))
-    for i in range(4):
-        mine = pl.ds(pl.multiple_of((2 * i + c) * 128, 128), 128)
-        copy = pltpu.make_async_copy(
-            down.at[:, mine], W.at[x, y, z, own_rows, pl.ds(i * 128, 128)], wl.at[i]
-        )
-        copy.start()
-        w_local.append(copy)
+    def ychunk(q):
+        yy = lax.rem(y + (0, 3, 1, 2)[q], 4)
+        return pl.ds(pl.multiple_of(yy * 2048, 2048), 2048)
+
+    hlocal = [
+        pltpu.make_async_copy(hid.at[:, ychunk(q)], H.at[0, :, ychunk(q)], lsem.at[q])
+        for q in range(4)
+    ]
+    ocopy = pltpu.make_async_copy(outp, OP, lsem.at[5])
+
     hremote = [
         remote(hid.at[:, ychunk(q)], H.at[1, :, ychunk(q)], hs.at[q], hr.at[q], core_dev)
         for q in range(4)
     ]
-    go(hremote[0])
-    m_kv = [go(message(kv.at[c], kvb.at[z], z_dev[d])) for d in range(3)]
+    m_kv = [go(message(ku.at[c], kub.at[z], z_dev[d])) for d in range(3)]
+    m_kv += [go(message(vu.at[c], vub.at[z], z_dev[d])) for d in range(3)]
 
     in_plane = pl.ds(pl.multiple_of(s * 64, 64), 192)
     prow = pl.ds(pl.multiple_of(s * 224, 32), 32)
@@ -262,6 +308,11 @@
     for m in (0, 2):
         a_piece(m).start()
         b_piece(0, m).start()
+    for q in (0, 1):
+        go(hremote[q])
+    for copy in hlocal:
+        copy.start()
+    ocopy.start()
 
     m_pick.wait_recv()
     both = (picked[...].astype(F32) + pickb[...].astype(F32)).astype(BF)
@@ -281,9 +332,9 @@
             )
             part[cc, i, :, 1152:1280] = squares
     m_core = go(message(part.at[o], rcore, core_dev))
-    m_tab = go(message(tab, ptab, core_dev))
-    m_bias = go(message(bias_b, pbias, core_dev))
-    for q in (1, 2, 3):
+    m_tab = go(message(page, ppage, core_dev))
+    m_bias = go(message(bias.at[1], pbias, core_dev))
+    for q in (2, 3):
         go(hremote[q])
 
     m_cross.wait_recv()
@@ -296,8 +347,6 @@
     b_piece(1, 0).start()
     b_piece(1, 2).start()
     a_piece(2).wait_recv()
-    b_piece(2, 0).start()
-    b_piece(2, 2).start()
 
     m_core.wait_recv()
     for i in range(4):
@@ -312,8 +361,6 @@
     side_start(1, 0)
     a_piece(3).wait_recv()
     a_piece(5).start()
-    b_piece(2, 1).start()
-    b_piece(2, 3).start()
     side_start(2, 0)
 
     for m in m_z:
@@ -321,14 +368,6 @@
     rz[3] = qsum[z] + rz[0] + rz[1] + rz[2]
     m_y = [go(message(rz.at[3], ry.at[d - 1], y_dev[d - 1])) for d in (1, 2, 3)]
 
-    a_piece(4).wait_recv()
-    b_piece(3, 0).start()
-    b_piece(3, 2).start()
-    a_piece(5).wait_recv()
-    b_piece(3, 1).start()
-    b_piece(3, 3).start()
-    side_start(3, 0)
-
     for m in m_y:
         m.wait_recv()
     ry[3] = rz[3] + ry[0] + ry[1] + ry[2]
@@ -339,6 +378,10 @@
 
     m_q = [message(qz.at[z], qz.at[z], z_dev[d - 1]) for d in (1, 2, 3)]
     sent.extend(m_q)
+
+    line = lax.broadcasted_iota(jnp.int32, (128, 128), 0)
+    lane = lax.broadcasted_iota(jnp.int32, (128, 128), 1)
+    lane16 = lax.broadcasted_iota(jnp.int32, (16, 128), 1)
 
     def step(n, carry):
         for k in range(4):
@@ -352,6 +395,13 @@
                 side_start(k, 1)
                 b_piece(k, 2).wait_recv()
                 side_start(k, 2)
+                if k == 0:
+                    a_piece(4).wait_recv()
+                    a_piece(5).wait_recv()
+                    side_start(3, 0)
+                if k < 2:
+                    for m in range(4):
+                        b_piece(k + 2, m).start()
 
             @pl.when(n == PART2[k])
             def _():
@@ -375,7 +425,52 @@
             for m in m_q:
                 m.start()
 
-        for q, at in enumerate((0, 1, 3, 5)):
+        @pl.when(n == 4)
+        def _():
+            m_tab.wait_recv()
+            m_bias.wait_recv()
+            pbias[...] = pbias[...] + bias[0]
+            cos_b = page[64:80, 0:HD]
+            sin_b = page[64:80, HD : 2 * HD]
+            sign = jnp.where(lane16 < HD // 2, -1.0, 1.0)
+            for t in range(2):
+                ref = ppage if t else page
+                for p in range(48):
+                    cos_a = ref[p : p + 1, 0:HD]
+                    sin_a = ref[p : p + 1, HD : 2 * HD]
+                    tabs[t, p * 16 : (p + 1) * 16, 0:HD] = cos_a * cos_b - sin_a * sin_b
+                    tabs[t, p * 16 : (p + 1) * 16, HD : 2 * HD] = (
+                        sin_a * cos_b + cos_a * sin_b
+                    ) * sign
+
+        @pl.when(n == 8)
+        def _():
+            for m in m_kv:
+                m.wait_recv()
+            kub[z] = ku[c]
+            vub[z] = vu[c]
+            for m in m_q:
+                m.wait_recv()
+            to_requests = (
+                lane == (line % 32) // 4 * 16 + line // 32 * 4 + line % 4
+            ).astype(F32).astype(BF)
+            pad = jnp.zeros((112, 128), BF)
+            for i in range(4):
+                Bm[i] = jnp.zeros((128, 256), BF)
+                Bm[i, 0:64, 0:128] = kub[i]
+                Bm[i, 64:128, 128:256] = vub[i]
+                heads = jnp.concatenate(
+                    [qz[i, :, j * 128 : (j + 1) * 128] for j in range(8)], axis=0
+                )
+                Q[i] = jnp.dot(to_requests, heads, preferred_element_type=F32).astype(BF)
+                fresh = jnp.dot(qz[i, :, 1024:1152], Bm[i], preferred_element_type=F32)
+                FK[i] = jnp.concatenate(
+                    [rope(fresh[:, 0:128], ftab[:, 0:128], ftab[:, 128:256]).astype(BF), pad],
+                    axis=0,
+                )
+                FV[i] = jnp.concatenate([fresh[:, 128:256].astype(BF), pad], axis=0)
+
+        for q, at in enumerate((0, 1, 2, 7)):
             @pl.when(n == at)
             def _():
                 hlocal[q].wait()
@@ -394,11 +489,9 @@
         def columns(xh, core):
             return pl.ds(pl.multiple_of((((yy * 2 + xh) * 2 + core) * 4 + zz) * 128, 128), 128)
 
-        def tile(m, carry):
-            t = m // 2
-            rows = pl.ds(pl.multiple_of((m % 2) * 384, 384), 384)
+        def tile(t, carry):
             left = [
-                jnp.concatenate([H[t, rows, columns(xh, 0)], H[t, rows, columns(xh, 1)]], axis=1)
+                jnp.concatenate([H[t, :, columns(xh, 0)], H[t, :, columns(xh, 1)]], axis=1)
                 for xh in (0, 1)
             ]
             product = jnp.dot(left[0], W[0, yy, zz], preferred_element_type=F32) + jnp.dot(
@@ -407,48 +500,18 @@
 
             @pl.when(n == 0)
             def _():
-                acc[t, rows, :] = product
+                acc[t] = product
 
             @pl.when(n > 0)
             def _():
-                acc[t, rows, :] += product
+                acc[t] += product
 
             return carry
 
-        lax.fori_loop(0, 4, tile, 0)
+        lax.fori_loop(0, 2, tile, 0)
         return carry
 
     lax.fori_loop(0, 16, step, 0)
-
-    for m in m_kv:
-        m.wait_recv()
-    kvb[z] = kv[c]
-    for m in m_q:
-        m.wait_recv()
-    m_tab.wait_recv()
-    m_bias.wait_recv()
-    pbias[...] = pbias[...] + bias_a[...]
-    line = lax.broadcasted_iota(jnp.int32, (128, 128), 0)
-    lane = lax.broadcasted_iota(jnp.int32, (128, 128), 1)
-    to_requests = (
-        lane == (line % 32) // 4 * 16 + line // 32 * 4 + line % 4
-    ).astype(F32).astype(BF)
-    to_heads = (
-        lane == (line % 16) // 4 * 32 + line // 16 * 4 + line % 4
-    ).astype(F32).astype(BF)
-    for i in range(4):
-        weights = kvb[i]
-        zero = jnp.zeros_like(weights)
-        Bm[i, :, 0:128] = jnp.where(line < 64, weights, zero)
-        Bm[i, :, 128:256] = jnp.where(line < 64, zero, weights)
-        heads = jnp.concatenate([qz[i, :, j * 128 : (j + 1) * 128] for j in range(8)], axis=0)
-        Q[i] = jnp.dot(to_requests, heads, preferred_element_type=F32).astype(BF)
-        fresh = jnp.dot(qz[i, :, 1024:1152], Bm[i], preferred_element_type=F32)
-        pad = jnp.zeros((112, 128), BF)
-        FK[i] = jnp.concatenate(
-            [rope(fresh[:, 0:128], ftab[:, 0:128], ftab[:, 128:256]).astype(BF), pad], axis=0
-        )
-        FV[i] = jnp.concatenate([fresh[:, 128:256].astype(BF), pad], axis=0)
 
     elsewhere = jnp.where((y + x + z) == 0, 0.0, masked_score)
     row32 = lax.broadcasted_iota(jnp.int32, (32, 128), 0)
@@ -457,8 +520,8 @@
 
     def request(r, carry):
         rows = pl.ds(pl.multiple_of(r * 192, 64), 192)
-        cosine = jnp.concatenate([tab[rows, 0:128], ptab[rows, 0:128]], axis=0)
-        sine = jnp.concatenate([tab[rows, 128:256], ptab[rows, 128:256]], axis=0)
+        cosine = jnp.concatenate([tabs[0, rows, 0:128], tabs[1, rows, 0:128]], axis=0)
+        sine = jnp.concatenate([tabs[0, rows, 128:256], tabs[1, rows, 128:256]], axis=0)
         seen = (col32 // 4 == r) & (col32 % 4 <= row32 % 4)
         mask = jnp.concatenate(
             [
@@ -490,40 +553,49 @@
             level = jnp.where(some, peak + jnp.log(safe), masked_score)
             at = pl.ds(pl.multiple_of(r * 32, 32), 32)
             ob[i, at, 0:128] = (context / safe).astype(BF)
-            ob[i, at, 128:256] = split_scalar(level)
+            lev[i, at, :] = jnp.broadcast_to(level, (32, HD))
         return carry
 
     lax.fori_loop(0, 4, request, 0)
 
+    for i in range(4):
+        ob[i, 128:144, :] = coded(lev[i, :, 0:1])
     m_cz = [
         go(message(ob.at[lax.rem(z + d, 4)], cz.at[d - 1], z_dev[d - 1])) for d in (1, 2, 3)
     ]
     for m in m_cz:
         m.wait_recv()
     value, level = merged([ob[z], cz[0], cz[1], cz[2]])
-    cmine[:, 0:128] = value.astype(BF)
-    cmine[:, 128:256] = split_scalar(level)
+    cmine[0:128] = value.astype(BF)
+    cmine[128:144] = coded(level)
     m_cy = [go(message(cmine, cy.at[d - 1], y_dev[d - 1])) for d in (1, 2, 3)]
     for m in m_cy:
         m.wait_recv()
     value, level = merged([cmine[...], cy[0], cy[1], cy[2]])
-    cmine2[:, 0:128] = value.astype(BF)
-    cmine2[:, 128:256] = split_scalar(level)
-    m_cx = go(message(cmine2, cx, xhi_dev))
-    m_cx.wait_recv()
-    value, _ = merged([cmine2[...], cx[...]])
-    ctx[c] = jnp.dot(to_heads, value.astype(BF), preferred_element_type=F32).astype(BF)
-    m_ctx = go(message(ctx.at[c], ctx.at[c], core_dev))
-    m_ctx.wait_recv()
+    cx[c, x, 0:128] = value.astype(BF)
+    cx[c, x, 128:144] = coded(level)
+    slot = cx.at[c, x]
+    m_cx = [go(message(slot, slot, device)) for device in (xhi_dev, core_dev, dev(x_=1 - x, c_=o))]
+    for m in m_cx:
+        m.wait_recv()
     ocopy.wait()
-    left = jnp.concatenate(
-        [ctx[g, j * 16 : (j + 1) * 16, :] for g in range(2) for j in range(8)], axis=1
-    )
-    fin[z] = jnp.dot(left, OP[...], preferred_element_type=F32)
+    to_heads = (
+        lane == (line % 16) // 4 * 32 + line // 16 * 4 + line % 4
+    ).astype(F32).astype(BF)
+    heads = []
+    for g in range(2):
+        value, _ = merged([cx[g, 0], cx[g, 1]])
+        moved = jnp.dot(to_heads, value.astype(BF), preferred_element_type=F32).astype(BF)
+        heads += [moved[j * 16 : (j + 1) * 16] for j in range(8)]
+    fin[z] = jnp.dot(
+        jnp.concatenate(heads, axis=1), OP[...], preferred_element_type=F32
+    ).astype(BF)
     m_fin = [go(message(fin.at[z], fin.at[z], z_dev[d - 1])) for d in (1, 2, 3)]
     for m in m_fin:
         m.wait_recv()
-    out_ref[...] = (fin[0] + fin[1] + fin[2] + fin[3]).astype(BF)
+    result = functools.reduce(jnp.add, [fin[d].astype(F32) for d in range(4)])
+    for r in range(4):
+        out_ref[r] = result[r * 4 : (r + 1) * 4].astype(BF)
 
     for copy in sent:
         copy.wait_send()
@@ -543,18 +615,18 @@
     lax.fori_loop(0, 4, drain, 0)
 
 
-MESSAGES = 1 + 3 + 3 + 3 + 3 + 1 + 3 + 3 + 3 + 1 + 1 + 3
-
-
-def main(hid, down, picked, qproj, kv, outp, tab, bias_a, bias_b, ftab):
+MESSAGES = 1 + 6 + 3 + 3 + 3 + 1 + 3 + 3 + 3 + 3 + 3
+
+
+def main(hid, down, picked, qproj, ku, vu, outp, page, bias, ftab):
     vm = pl.BlockSpec(memory_space=pltpu.VMEM)
     anyspace = pl.BlockSpec(memory_space=pl.ANY)
     V = pltpu.VMEM
     S = pltpu.SemaphoreType.DMA
     return pl.pallas_call(
         main_kernel,
-        out_shape=jax.ShapeDtypeStruct((16, 512), BF),
-        in_specs=[anyspace, vm, vm, anyspace, vm, anyspace, vm, vm, vm, vm],
+        out_shape=jax.ShapeDtypeStruct((4, 4, 512), BF),
+        in_specs=[anyspace, vm, vm, anyspace, vm, vm, anyspace, vm, vm, vm],
         out_specs=vm,
         scratch_shapes=[
             V((2, 768, 8192), BF),
@@ -562,8 +634,10 @@
             V((2, 768, 512), F32),
             V((128, 8192), BF),
             V((2048, 512), BF),
-            V((4, 128, 128), BF),
-            V((768, 256), F32),
+            V((4, 64, 128), BF),
+            V((4, 64, 128), BF),
+            V((2, 768, 256), F32),
+            V((80, 256), F32),
             V((8, 384), F32),
             V((32, 128), BF),
             V((2, 4, 16, 1280), F32),
@@ -577,14 +651,13 @@
             V((4, 128, 128), BF),
             V((4, 128, 128), BF),
             V((4, 128, 128), BF),
-            V((4, 128, 256), BF),
-            V((3, 128, 256), BF),
-            V((128, 256), BF),
-            V((3, 128, 256), BF),
-            V((128, 256), BF),
-            V((128, 256), BF),
-            V((2, 128, 128), BF),
-            V((4, 16, 512), F32),
+            V((4, 144, 128), BF),
+            V((4, 128, 128), F32),
+            V((3, 144, 128), BF),
+            V((144, 128), BF),
+            V((3, 144, 128), BF),
+            V((2, 2, 144, 128), BF),
+            V((4, 16, 512), BF),
             S((6,)),
             S((4,)),
             S((4,)),
@@ -603,16 +676,7 @@
             collective_id=0, has_side_effects=True, vmem_limit_bytes=62 * 2**20
         ),
         name="gather_decode",
-    )(hid, down, picked, qproj, kv, outp, tab, bias_a, bias_b, ftab)
-
-
-def rope_table(positions):
-    half = HD // 2
-    frequency = 1.0 / rope_base ** (jnp.arange(half, dtype=F32) * 2.0 / HD)
-    angles = positions.astype(F32)[:, None] * frequency
-    cosine = jnp.cos(angles)
-    sine = jnp.sin(angles)
-    return jnp.concatenate([cosine, cosine, -sine, sine], axis=1)
+    )(hid, down, picked, qproj, ku, vu, outp, page, bias, ftab)
 
 
 def local(
@@ -620,29 +684,13 @@
     query_proj, down_proj, key_up, value_up, out_proj,
 ):
     requests, span, width = cached_hidden.shape
-    steps = new_ids.shape[1]
-    pages = span // PAGE
-    picked = pick(new_ids, embedding)
-    run = lax.axis_index(SEQ_HEAD)
-    slots = jnp.arange(pages, dtype=jnp.int32)
-    logical = jnp.sum(
-        jnp.where(page_order[:, None, :] == slots[None, :, None], slots[None, None, :], 0), axis=2
+    frequency = 1.0 / rope_base ** (np.arange(HD // 2) * 2.0 / HD)
+    freq = jnp.asarray(np.tile(np.concatenate([frequency, frequency]), (8, 1)).astype(np.float32))
+    picked, page, fresh, bias = prepare(new_ids, page_order, lengths, freq, embedding)
+    return main(
+        cached_hidden.reshape(requests * span, width), down_proj, picked, query_proj, key_up,
+        value_up, out_proj, page, bias, fresh,
     )
-    positions = (
-        run * span + logical[:, :, None] * PAGE + jnp.arange(PAGE, dtype=jnp.int32)[None, None, :]
-    ).reshape(requests, span)
-    tab = rope_table(positions.reshape(-1))
-    bias = jnp.where(positions < lengths[:, None], 0.0, masked_score).astype(F32)
-    bias_a = jnp.pad(bias, ((0, 4), (0, span)))
-    bias_b = jnp.pad(bias, ((0, 4), (span, 0)))
-    fresh = (lengths[:, None] + jnp.arange(steps, dtype=jnp.int32)[None, :]).reshape(-1)
-    ftab = rope_table(fresh)
-    kv = jnp.concatenate([key_up, value_up], axis=1)
-    out = main(
-        cached_hidden.reshape(requests * span, width), down_proj, picked, query_proj, kv,
-        out_proj, tab, bias_a, bias_b, ftab,
-    )
-    return out.reshape(requests, steps, -1)
 
 
 def solution(mesh):

time: 123 us -> 102 us (0.83)
  Pallas kernels: 111 us -> 100 us
  other arithmetic: 7.43 us -> 0 us
  local copies, waits for them, and re-layouts: 3.86 us -> 1.33 us
    pallas_call x2, Pallas kernels: 111 us -> 100 us  [the longest x1 97.2 us: main(): pl.pallas_call(main_kernel, out_shape=jax.ShapeDtypeStruct((4, 4, 512), B...]
    concatenate x3 -> x0, other arithmetic: 3.35 us -> none  [the longest x2 1.94 us: rope_table(): return jnp.concatenate([cosine, cosine, -sine, sine], axis=1)]
    cos x2 -> x0, other arithmetic: 1.57 us -> none  [rope_table(): cosine = jnp.cos(angles)]
    reshape x1 -> x0, local copies, waits for them, and re-layouts: 1.33 us -> none  [local(): return out.reshape(requests, steps, -1)]
where the time goes in v2:
time: 102 us; the launch traced here: 101 us
  Pallas kernels  100 us (98%)
  local copies, waits for them, and re-layouts  1.33 us (1%)
    pallas_call x1, Pallas kernels, main(): pl.pallas_call(main_kernel, out_shape=jax.ShapeDtypeStruct((4, 4, 512), B...  97.2 us
    pallas_call x1, Pallas kernels, prepare(): pl.pallas_call(prepare_kernel, out_shape=(jax.ShapeDtypeStruct((count, HD...  2.92 us

profile of v2, /device:TPU:1, one launch (start us, length us, event | category | flops | bytes accessed | tf_op | source)
XLA Modules:
  0.0 101.5 jit_solution(8988295098816527052)
XLA Ops:
  0.0 2.9 %prepare.1 = (bf16[32,128]{1,0:T(8,128)(2,1)}, f32[80,256]{1,0:T(8,128)}, f32[16,256]{1,0:T(8,128)}, f32[2,8,384]{2,1,0:T(8,128)}) custom-call(s32[4,8]{1,0:T(4,128)} %bitcast.3, s32[4,12]{1,0:T(4,128)} %order_ref.1, s32[4]{0:T(128)} %lengths_ref.1, f32[8,128]{1,0:T(8,128)} %constant.2.clone.freq_ref, bf16[32256,128]{1,0:T(8,128)(2,1)} %emb_ref.1), custom_call_target="tpu_custom_call" | custom-call | tf_op jit(solution)/shard_map/prepare/pallas_call | solution.py:91
  2.9 97.2 %gather_decode.1 = bf16[4,4,512]{2,1,0:T(4,128)(2,1)} custom-call(bf16[768,8192]{1,0:T(8,128)(2,1)} %bitcast.2, bf16[128,1024]{1,0:T(8,128)(2,1)} %down.1, bf16[32,128]{1,0:T(8,128)(2,1)} %get-tuple-element.9.picked, bf16[128,8192]{1,0:T(8,128)(2,1)} %qproj.1, bf16[2,64,128]{2,1,0:T(8,128)(2,1)} %ku.1, bf16[2,64,128]{2,1,0:T(8,128)(2,1)} %vu.1, ...), custom_call_target="tpu_custom_call" | custom-call | tf_op jit(solution)/shard_map/gather_decode/pallas_call | solution.py:626
  100.1 1.3 %copy.13 = bf16[4,4,512]{2,1,0:T(4,128)(2,1)} copy(bf16[4,4,512]{2,1,0:T(4,128)(2,1)} %gather_decode.1) | data formatting | bytes 32768

commit v3 on v2

--- a/solution.py
+++ b/solution.py
@@ -148,10 +148,10 @@
 
 STEPS = (
     (0, 0), (1, 0), (2, 0), (0, 1), (0, 2), (1, 1), (1, 2), (3, 0),
-    (2, 1), (2, 2), (3, 1), (3, 2), (0, 3), (1, 3), (2, 3), (3, 3),
+    (0, 3), (2, 1), (2, 2), (1, 3), (3, 1), (3, 2), (2, 3), (3, 3),
 )
 PART1 = (1, 3, 5, 7)
-PART2 = (9, 10, 11, 12)
+PART2 = (5, 7, 9, 10)
 
 
 def pick_int(n, values):
@@ -298,6 +298,8 @@
     def side_start(k, b):
         side_piece(k, b, 0).start()
         side_piece(k, b, 1).start()
+
+    acc[...] = jnp.zeros_like(acc)
 
     for copy in w_local:
         copy.wait()
@@ -337,24 +339,17 @@
     for q in (2, 3):
         go(hremote[q])
 
-    m_cross.wait_recv()
-    for m in (1, 3):
-        a_piece(m).start()
-        b_piece(0, m).start()
-
     a_piece(0).wait_recv()
     a_piece(4).start()
     b_piece(1, 0).start()
     b_piece(1, 2).start()
     a_piece(2).wait_recv()
-
-    m_core.wait_recv()
-    for i in range(4):
-        qsum[i] = part[c, i] + rcore[i]
-    m_z = [
-        go(message(qsum.at[lax.rem(z + d, 4)], rz.at[d - 1], z_dev[d - 1])) for d in (1, 2, 3)
-    ]
-
+    b_piece(2, 0).start()
+    b_piece(2, 2).start()
+    m_cross.wait_recv()
+    for m in (1, 3):
+        a_piece(m).start()
+        b_piece(0, m).start()
     a_piece(1).wait_recv()
     b_piece(1, 1).start()
     b_piece(1, 3).start()
@@ -363,15 +358,12 @@
     a_piece(5).start()
     side_start(2, 0)
 
-    for m in m_z:
-        m.wait_recv()
-    rz[3] = qsum[z] + rz[0] + rz[1] + rz[2]
-    m_y = [go(message(rz.at[3], ry.at[d - 1], y_dev[d - 1])) for d in (1, 2, 3)]
-
-    for m in m_y:
-        m.wait_recv()
-    ry[3] = rz[3] + ry[0] + ry[1] + ry[2]
-    m_x = go(message(ry.at[3], rx, xhi_dev))
+    m_z = [
+        message(qsum.at[lax.rem(z + d, 4)], rz.at[d - 1], z_dev[d - 1]) for d in (1, 2, 3)
+    ]
+    m_y = [message(rz.at[3], ry.at[d - 1], y_dev[d - 1]) for d in (1, 2, 3)]
+    m_x = message(ry.at[3], rx, xhi_dev)
+    sent.extend(m_z + m_y + [m_x])
 
     lines = [st[0] for st in STEPS]
     places = [st[1] for st in STEPS]
@@ -396,12 +388,16 @@
                 b_piece(k, 2).wait_recv()
                 side_start(k, 2)
                 if k == 0:
+                    b_piece(2, 1).start()
+                    b_piece(2, 3).start()
+                if k == 1:
                     a_piece(4).wait_recv()
+                    b_piece(3, 0).start()
+                    b_piece(3, 2).start()
                     a_piece(5).wait_recv()
+                    b_piece(3, 1).start()
+                    b_piece(3, 3).start()
                     side_start(3, 0)
-                if k < 2:
-                    for m in range(4):
-                        b_piece(k + 2, m).start()
 
             @pl.when(n == PART2[k])
             def _():
@@ -409,7 +405,30 @@
                 b_piece(k, 5).wait_recv()
                 side_start(k, 3)
 
-        @pl.when(n == 1)
+        @pl.when(n == 0)
+        def _():
+            m_core.wait_recv()
+            for i in range(4):
+                qsum[i] = part[c, i] + rcore[i]
+            for m in m_z:
+                m.start()
+
+        @pl.when(n == 2)
+        def _():
+            for m in m_z:
+                m.wait_recv()
+            rz[3] = qsum[z] + rz[0] + rz[1] + rz[2]
+            for m in m_y:
+                m.start()
+
+        @pl.when(n == 4)
+        def _():
+            for m in m_y:
+                m.wait_recv()
+            ry[3] = rz[3] + ry[0] + ry[1] + ry[2]
+            m_x.start()
+
+        @pl.when(n == 6)
         def _():
             m_x.wait_recv()
             total = ry[3] + rx[...]
@@ -425,7 +444,7 @@
             for m in m_q:
                 m.start()
 
-        @pl.when(n == 4)
+        @pl.when(n == 8)
         def _():
             m_tab.wait_recv()
             m_bias.wait_recv()
@@ -443,7 +462,7 @@
                         sin_a * cos_b + cos_a * sin_b
                     ) * sign
 
-        @pl.when(n == 8)
+        @pl.when(n == 11)
         def _():
             for m in m_kv:
                 m.wait_recv()
@@ -498,14 +517,7 @@
                 left[1], W[1, yy, zz], preferred_element_type=F32
             )
 
-            @pl.when(n == 0)
-            def _():
-                acc[t] = product
-
-            @pl.when(n > 0)
-            def _():
-                acc[t] += product
-
+            acc[t] += product
             return carry
 
         lax.fori_loop(0, 2, tile, 0)
@@ -518,31 +530,39 @@
     col32 = lax.broadcasted_iota(jnp.int32, (32, 128), 1)
     scaling = 1.0 / math.sqrt(HD)
 
-    def request(r, carry):
-        rows = pl.ds(pl.multiple_of(r * 192, 64), 192)
-        cosine = jnp.concatenate([tabs[0, rows, 0:128], tabs[1, rows, 0:128]], axis=0)
-        sine = jnp.concatenate([tabs[0, rows, 128:256], tabs[1, rows, 128:256]], axis=0)
-        seen = (col32 // 4 == r) & (col32 % 4 <= row32 % 4)
-        mask = jnp.concatenate(
-            [
-                jnp.broadcast_to(pbias[pl.ds(r, 1), :], (32, 384)),
-                jnp.where(seen, elsewhere, masked_score),
-            ],
-            axis=1,
+    first_cz = ex[0]
+    ex[0] += 3
+
+    def partial_message(step):
+        i = lax.rem(z + 1 + step, 4)
+        return remote(
+            ob.at[i], cz.at[step], es.at[first_cz + step], er.at[first_cz + step], dev(z_=i)
         )
-        for i in range(4):
-            latent = jnp.concatenate(
-                [acc[0, rows, i * 128 : (i + 1) * 128], acc[1, rows, i * 128 : (i + 1) * 128]],
-                axis=0,
-            ).astype(BF)
+
+    def group(step, carry):
+        i = lax.rem(z + 1 + step, 4)
+        lanes = pl.ds(pl.multiple_of(i * 128, 128), 128)
+        for r in range(4):
+            rows = slice(r * 192, (r + 1) * 192)
+            at = slice(r * 32, (r + 1) * 32)
+            seen = (col32 // 4 == r) & (col32 % 4 <= row32 % 4)
+            mask = jnp.concatenate(
+                [
+                    jnp.broadcast_to(pbias[r : r + 1, :], (32, 384)),
+                    jnp.where(seen, elsewhere, masked_score),
+                ],
+                axis=1,
+            )
+            latent = jnp.concatenate([acc[0, rows, lanes], acc[1, rows, lanes]], axis=0).astype(BF)
             rebuilt = jnp.dot(latent, Bm[i], preferred_element_type=F32)
+            cosine = jnp.concatenate([tabs[0, rows, 0:128], tabs[1, rows, 0:128]], axis=0)
+            sine = jnp.concatenate([tabs[0, rows, 128:256], tabs[1, rows, 128:256]], axis=0)
             keys = jnp.concatenate(
                 [rope(rebuilt[:, 0:128], cosine, sine).astype(BF), FK[i]], axis=0
             )
             values = jnp.concatenate([rebuilt[:, 128:256].astype(BF), FV[i]], axis=0)
-            query = Q[i, pl.ds(pl.multiple_of(r * 32, 32), 32), :]
             scores = lax.dot_general(
-                query, keys, (((1,), (1,)), ((), ())), preferred_element_type=F32
+                Q[i, at, :], keys, (((1,), (1,)), ((), ())), preferred_element_type=F32
             ) * scaling + mask
             peak = jnp.max(scores, axis=1, keepdims=True)
             e = jnp.where(mask > -1e29, jnp.exp(scores - peak), 0.0)
@@ -551,18 +571,20 @@
             some = total > 0.0
             safe = jnp.where(some, total, 1.0)
             level = jnp.where(some, peak + jnp.log(safe), masked_score)
-            at = pl.ds(pl.multiple_of(r * 32, 32), 32)
-            ob[i, at, 0:128] = (context / safe).astype(BF)
-            lev[i, at, :] = jnp.broadcast_to(level, (32, HD))
+            ob[i, at, :] = (context / safe).astype(BF)
+            lev[at, :] = jnp.broadcast_to(level, (32, HD))
+        ob[i, 128:144, :] = coded(lev[:, 0:1])
+
+        @pl.when(step < 3)
+        def _():
+            partial_message(step).start()
+
         return carry
 
-    lax.fori_loop(0, 4, request, 0)
-
-    for i in range(4):
-        ob[i, 128:144, :] = coded(lev[i, :, 0:1])
-    m_cz = [
-        go(message(ob.at[lax.rem(z + d, 4)], cz.at[d - 1], z_dev[d - 1])) for d in (1, 2, 3)
-    ]
+    lax.fori_loop(0, 4, group, 0)
+
+    m_cz = [partial_message(d) for d in range(3)]
+    sent.extend(m_cz)
     for m in m_cz:
         m.wait_recv()
     value, level = merged([ob[z], cz[0], cz[1], cz[2]])
@@ -652,7 +674,7 @@
             V((4, 128, 128), BF),
             V((4, 128, 128), BF),
             V((4, 144, 128), BF),
-            V((4, 128, 128), F32),
+            V((128, 128), F32),
             V((3, 144, 128), BF),
             V((144, 128), BF),
             V((3, 144, 128), BF),

time: 102 us -> 92.2 us (0.904)
  Pallas kernels: 100 us -> 90.6 us
    pallas_call x1, Pallas kernels: 97.2 us -> 87.5 us  [main(): pl.pallas_call(main_kernel, out_shape=jax.ShapeDtypeStruct((4, 4, 512), B...]
where the time goes in v3:
time: 92.2 us; the launch traced here: 92 us
  Pallas kernels  90.6 us (98%)
  local copies, waits for them, and re-layouts  1.33 us (1%)
    pallas_call x1, Pallas kernels, main(): pl.pallas_call(main_kernel, out_shape=jax.ShapeDtypeStruct((4, 4, 512), B...  87.5 us
    pallas_call x1, Pallas kernels, prepare(): pl.pallas_call(prepare_kernel, out_shape=(jax.ShapeDtypeStruct((count, HD...  3.15 us

profile of v3, /device:TPU:1, one launch (start us, length us, event | category | flops | bytes accessed | tf_op | source)
XLA Modules:
  0.0 92.0 jit_solution(9835578606377191503)
XLA Ops:
  0.0 3.2 %prepare.1 = (bf16[32,128]{1,0:T(8,128)(2,1)}, f32[80,256]{1,0:T(8,128)}, f32[16,256]{1,0:T(8,128)}, f32[2,8,384]{2,1,0:T(8,128)}) custom-call(s32[4,8]{1,0:T(4,128)} %bitcast.3, s32[4,12]{1,0:T(4,128)} %order_ref.1, s32[4]{0:T(128)} %lengths_ref.1, f32[8,128]{1,0:T(8,128)} %constant.2.clone.freq_ref, bf16[32256,128]{1,0:T(8,128)(2,1)} %emb_ref.1), custom_call_target="tpu_custom_call" | custom-call | tf_op jit(solution)/shard_map/prepare/pallas_call | solution.py:91
  3.2 87.5 %gather_decode.1 = bf16[4,4,512]{2,1,0:T(4,128)(2,1)} custom-call(bf16[768,8192]{1,0:T(8,128)(2,1)} %bitcast.2, bf16[128,1024]{1,0:T(8,128)(2,1)} %down.1, bf16[32,128]{1,0:T(8,128)(2,1)} %get-tuple-element.9.picked, bf16[128,8192]{1,0:T(8,128)(2,1)} %qproj.1, bf16[2,64,128]{2,1,0:T(8,128)(2,1)} %ku.1, bf16[2,64,128]{2,1,0:T(8,128)(2,1)} %vu.1, ...), custom_call_target="tpu_custom_call" | custom-call | tf_op jit(solution)/shard_map/gather_decode/pallas_call | solution.py:648
  90.6 1.3 %copy.13 = bf16[4,4,512]{2,1,0:T(4,128)(2,1)} copy(bf16[4,4,512]{2,1,0:T(4,128)(2,1)} %gather_decode.1) | data formatting | bytes 32768

commit v4 on v3

--- a/solution.py
+++ b/solution.py
@@ -147,11 +147,11 @@
 
 
 STEPS = (
-    (0, 0), (1, 0), (2, 0), (0, 1), (0, 2), (1, 1), (1, 2), (3, 0),
-    (0, 3), (2, 1), (2, 2), (1, 3), (3, 1), (3, 2), (2, 3), (3, 3),
+    (0, 0), (1, 0), (2, 0), (0, 1), (0, 2), (1, 1), (1, 2), (2, 1),
+    (2, 2), (3, 0), (0, 3), (1, 3), (3, 1), (3, 2), (2, 3), (3, 3),
 )
 PART1 = (1, 3, 5, 7)
-PART2 = (5, 7, 9, 10)
+PART2 = (7, 9, 10, 12)
 
 
 def pick_int(n, values):
@@ -166,8 +166,9 @@
 
 
 def main_kernel(
-    hid, down, picked, qproj, ku, vu, outp, page, bias, ftab,
+    hid, down_h, picked_h, qproj, ku, vu, outp, page_h, bias_h, ftab_h,
     out_ref,
+    down, picked, page, bias, ftab,
     H, W, acc, QP, OP, kub, vub, tabs, ppage, pbias, pickb, part, rcore, qsum, rz, ry, rx, qz,
     Bm, FK, FV, Q, ob, lev, cz, cmine, cy, cx, fin,
     lsem, wl, hs, hr, ws, wr, xs, ps, pr, fs, fr, es, er,
@@ -191,22 +192,34 @@
             device_id=device, device_id_type=MESH,
         )
 
+    everyone = [core_dev, pair_dev, cross_dev, xhi_dev, dev(x_=1 - x, c_=o)] + z_dev + y_dev
+    barrier = pltpu.get_barrier_semaphore()
+    for device in everyone:
+        pl.semaphore_signal(barrier, inc=1, device_id=device, device_id_type=MESH)
+
     own_rows = pl.ds(pl.multiple_of(c * 128, 128), 128)
     w_local = []
     for i in range(4):
         mine = pl.ds(pl.multiple_of((2 * i + c) * 128, 128), 128)
         copy = pltpu.make_async_copy(
-            down.at[:, mine], W.at[x, y, z, own_rows, pl.ds(i * 128, 128)], wl.at[i]
+            down_h.at[:, mine], W.at[x, y, z, own_rows, pl.ds(i * 128, 128)], wl.at[i]
         )
         copy.start()
         w_local.append(copy)
+    small = [
+        pltpu.make_async_copy(src, dst, lsem.at[6 + k])
+        for k, (src, dst) in enumerate(
+            [
+                (picked_h, picked), (down_h, down), (ftab_h, ftab), (page_h, page),
+                (bias_h, bias), (ku.at[c], kub.at[z]), (vu.at[c], vub.at[z]),
+            ]
+        )
+    ]
+    for copy in small:
+        copy.start()
     qcopy = pltpu.make_async_copy(qproj, QP, lsem.at[4])
     qcopy.start()
 
-    everyone = [core_dev, pair_dev, cross_dev, xhi_dev, dev(x_=1 - x, c_=o)] + z_dev + y_dev
-    barrier = pltpu.get_barrier_semaphore()
-    for device in everyone:
-        pl.semaphore_signal(barrier, inc=1, device_id=device, device_id_type=MESH)
     pl.semaphore_wait(barrier, len(everyone))
 
     sent = []
@@ -223,12 +236,12 @@
         ex[0] += 1
         return remote(src, dst, es.at[k], er.at[k], device)
 
-    m_pick = go(message(picked, pickb, pair_dev))
+    m_pick = go(message(picked_h, pickb, pair_dev))
     w_init = []
     for i in range(4):
         theirs = pl.ds(pl.multiple_of((2 * i + o) * 128, 128), 128)
         w_init.append(go(remote(
-            down.at[:, theirs], W.at[x, y, z, own_rows, pl.ds(i * 128, 128)],
+            down_h.at[:, theirs], W.at[x, y, z, own_rows, pl.ds(i * 128, 128)],
             ws.at[i], wr.at[i], core_dev,
         )))
     def ychunk(q):
@@ -317,6 +330,8 @@
     ocopy.start()
 
     m_pick.wait_recv()
+    small[0].wait()
+    small[1].wait()
     both = (picked[...].astype(F32) + pickb[...].astype(F32)).astype(BF)
     pickb[...] = both
     rows16 = pickb[pl.ds(pl.multiple_of(s * 16, 16), 16), :]
@@ -334,8 +349,8 @@
             )
             part[cc, i, :, 1152:1280] = squares
     m_core = go(message(part.at[o], rcore, core_dev))
-    m_tab = go(message(page, ppage, core_dev))
-    m_bias = go(message(bias.at[1], pbias, core_dev))
+    m_tab = go(message(page_h, ppage, core_dev))
+    m_bias = go(message(bias_h.at[1], pbias, core_dev))
     for q in (2, 3):
         go(hremote[q])
 
@@ -346,17 +361,12 @@
     a_piece(2).wait_recv()
     b_piece(2, 0).start()
     b_piece(2, 2).start()
+    b_piece(0, 0).wait_recv()
+    b_piece(0, 4).start()
     m_cross.wait_recv()
     for m in (1, 3):
         a_piece(m).start()
         b_piece(0, m).start()
-    a_piece(1).wait_recv()
-    b_piece(1, 1).start()
-    b_piece(1, 3).start()
-    side_start(1, 0)
-    a_piece(3).wait_recv()
-    a_piece(5).start()
-    side_start(2, 0)
 
     m_z = [
         message(qsum.at[lax.rem(z + d, 4)], rz.at[d - 1], z_dev[d - 1]) for d in (1, 2, 3)
@@ -376,13 +386,27 @@
     lane16 = lax.broadcasted_iota(jnp.int32, (16, 128), 1)
 
     def step(n, carry):
+        @pl.when(n == 1)
+        def _():
+            a_piece(1).wait_recv()
+            b_piece(1, 1).start()
+            b_piece(1, 3).start()
+            side_start(1, 0)
+            a_piece(3).wait_recv()
+            a_piece(5).start()
+            side_start(2, 0)
+
         for k in range(4):
             @pl.when(n == PART1[k])
             def _():
-                b_piece(k, 0).wait_recv()
-                b_piece(k, 4).start()
+                if k == 3:
+                    b_piece(3, 0).wait_recv()
+                    b_piece(3, 4).start()
                 b_piece(k, 3).wait_recv()
                 b_piece(k, 5).start()
+                if k < 2:
+                    b_piece(k + 1, 0).wait_recv()
+                    b_piece(k + 1, 4).start()
                 b_piece(k, 1).wait_recv()
                 side_start(k, 1)
                 b_piece(k, 2).wait_recv()
@@ -431,6 +455,7 @@
         @pl.when(n == 6)
         def _():
             m_x.wait_recv()
+            small[2].wait()
             total = ry[3] + rx[...]
             inverse = lax.rsqrt(
                 jnp.sum(total[:, 1152:1280], axis=1, keepdims=True) / D + 1e-05
@@ -447,6 +472,8 @@
         @pl.when(n == 8)
         def _():
             m_tab.wait_recv()
+            small[3].wait()
+            small[4].wait()
             m_bias.wait_recv()
             pbias[...] = pbias[...] + bias[0]
             cos_b = page[64:80, 0:HD]
@@ -466,8 +493,8 @@
         def _():
             for m in m_kv:
                 m.wait_recv()
-            kub[z] = ku[c]
-            vub[z] = vu[c]
+            small[5].wait()
+            small[6].wait()
             for m in m_q:
                 m.wait_recv()
             to_requests = (
@@ -489,7 +516,7 @@
                 )
                 FV[i] = jnp.concatenate([fresh[:, 128:256].astype(BF), pad], axis=0)
 
-        for q, at in enumerate((0, 1, 2, 7)):
+        for q, at in enumerate((0, 1, 2, 9)):
             @pl.when(n == at)
             def _():
                 hlocal[q].wait()
@@ -509,14 +536,11 @@
             return pl.ds(pl.multiple_of((((yy * 2 + xh) * 2 + core) * 4 + zz) * 128, 128), 128)
 
         def tile(t, carry):
-            left = [
-                jnp.concatenate([H[t, :, columns(xh, 0)], H[t, :, columns(xh, 1)]], axis=1)
-                for xh in (0, 1)
-            ]
-            product = jnp.dot(left[0], W[0, yy, zz], preferred_element_type=F32) + jnp.dot(
-                left[1], W[1, yy, zz], preferred_element_type=F32
+            left = jnp.concatenate(
+                [H[t, :, columns(xh, core)] for xh in (0, 1) for core in (0, 1)], axis=1
             )
-
+            right = jnp.concatenate([W[0, yy, zz], W[1, yy, zz]], axis=0)
+            product = jnp.dot(left, right, preferred_element_type=F32)
             acc[t] += product
             return carry
 
@@ -648,9 +672,14 @@
     return pl.pallas_call(
         main_kernel,
         out_shape=jax.ShapeDtypeStruct((4, 4, 512), BF),
-        in_specs=[anyspace, vm, vm, anyspace, vm, vm, anyspace, vm, vm, vm],
+        in_specs=[anyspace] * 10,
         out_specs=vm,
         scratch_shapes=[
+            V((128, 1024), BF),
+            V((32, 128), BF),
+            V((80, 256), F32),
+            V((2, 8, 384), F32),
+            V((16, 256), F32),
             V((2, 768, 8192), BF),
             V((2, 4, 4, 256, 512), BF),
             V((2, 768, 512), F32),
@@ -680,7 +709,7 @@
             V((3, 144, 128), BF),
             V((2, 2, 144, 128), BF),
             V((4, 16, 512), BF),
-            S((6,)),
+            S((13,)),
             S((4,)),
             S((4,)),
             S((4,)),

time: 92.2 us -> 89.7 us (0.973)
  Pallas kernels: 90.6 us -> 88 us
    pallas_call x1, Pallas kernels: 87.5 us -> 85 us  [main(): pl.pallas_call(main_kernel, out_shape=jax.ShapeDtypeStruct((4, 4, 512), B...]
where the time goes in v4:
time: 89.7 us; the launch traced here: 89.4 us
  Pallas kernels  88 us (98%)
  local copies, waits for them, and re-layouts  1.33 us (1%)
    pallas_call x1, Pallas kernels, main(): pl.pallas_call(main_kernel, out_shape=jax.ShapeDtypeStruct((4, 4, 512), B...  85 us
    pallas_call x1, Pallas kernels, prepare(): pl.pallas_call(prepare_kernel, out_shape=(jax.ShapeDtypeStruct((count, HD...  3.03 us

profile of v4, /device:TPU:1, one launch (start us, length us, event | category | flops | bytes accessed | tf_op | source)
XLA Modules:
  0.0 89.4 jit_solution(547159602734413026)
XLA Ops:
  0.0 3.0 %prepare.1 = (bf16[32,128]{1,0:T(8,128)(2,1)}, f32[80,256]{1,0:T(8,128)}, f32[16,256]{1,0:T(8,128)}, f32[2,8,384]{2,1,0:T(8,128)}) custom-call(s32[4,8]{1,0:T(4,128)} %bitcast.3, s32[4,12]{1,0:T(4,128)} %order_ref.1, s32[4]{0:T(128)} %lengths_ref.1, f32[8,128]{1,0:T(8,128)} %constant.2.clone.freq_ref, bf16[32256,128]{1,0:T(8,128)(2,1)} %emb_ref.1), custom_call_target="tpu_custom_call" | custom-call | tf_op jit(solution)/shard_map/prepare/pallas_call | solution.py:91
  3.0 85.0 %gather_decode.1 = bf16[4,4,512]{2,1,0:T(4,128)(2,1)} custom-call(bf16[768,8192]{1,0:T(8,128)(2,1)} %bitcast.2, bf16[128,1024]{1,0:T(8,128)(2,1)} %down_h.1, bf16[32,128]{1,0:T(8,128)(2,1)} %get-tuple-element.9.picked_h, bf16[128,8192]{1,0:T(8,128)(2,1)} %qproj.1, bf16[2,64,128]{2,1,0:T(8,128)(2,1)} %ku.1, bf16[2,64,128]{2,1,0:T(8,128)(2,1)} %vu.1, ...), custom_call_target="tpu_custom_call" | custom-call | tf_op jit(solution)/shard_map/gather_decode/pallas_call | solution.py:672
  88.0 1.3 %copy.13 = bf16[4,4,512]{2,1,0:T(4,128)(2,1)} copy(bf16[4,4,512]{2,1,0:T(4,128)(2,1)} %gather_decode.1) | data formatting | bytes 32768
